TPU v7x, 256 devices: a whole 4x4x8 slice. The times are simulated.
256 devices in a mesh: seqhi: 16 (over x, z_lo, core), seqlo: 16 (over z_hi, y).
Axes of the slice: x: 4, y: 4, z: 8 (z_hi: 4, z_lo: 2; z = z_hi * 2 + z_lo), core: 2. Of those that a mesh axis runs over, the one named last changes fastest.
Arguments:
- queries: bfloat16 [65536, 2048], P(('seqhi', 'seqlo')), may hold values from -6 to 6
- keys: bfloat16 [65536, 128], P(('seqhi', 'seqlo')), may hold values from -6 to 6
- values: bfloat16 [65536, 128], P(('seqhi', 'seqlo')), may hold values from -6 to 6
- outputs: bfloat16 [65536, 2048], P(('seqhi', 'seqlo')), may hold values from -6 to 6
- out_grad: bfloat16 [65536, 2048], P(('seqhi', 'seqlo')), may hold values from -96 to 96
- lse: float32 [16, 65536], P(None, ('seqhi', 'seqlo')), may hold values from 7 to 9
- sink_keys: bfloat16 [128, 128], replicated, may hold values from -6 to 6
- sink_values: bfloat16 [128, 128], replicated, may hold values from -6 to 6
- window_len: int32 [16], replicated, may hold values from 256 to 2048, as said below
- sink_live: int32 [16], replicated, may hold values from 32 to 128, as said below
Outputs:
- query_grad: float32 [65536, 2048], P(('seqhi', 'seqlo'))
- key_grad: float32 [65536, 128], P(('seqhi', 'seqlo'))
- value_grad: float32 [65536, 128], P(('seqhi', 'seqlo'))
- sink_key_grad: float32 [128, 128], replicated
- sink_value_grad: float32 [128, 128], replicated
Inputs may be any that keep to these rules, and one draw needn't show every extreme that they name: `window_len`: one head's window is exactly 2048. `sink_live`: one head reads all 128 initial keys.
All inputs are finite; a program needn't handle non-finite values.
Results may differ from a plain program's by a relative error of at most 0.0039.
Values may be sent and summed in bfloat16 or wider, within the bound.
A program may use at most 64 MiB of HBM per device.

v0:
```python
import jax
import jax.numpy as jnp
from jax import lax
from jax.sharding import PartitionSpec as P

WIN = 2048


def shifted(block, axis, distance):
    devices = range(lax.axis_size(axis))
    route = [(i - distance, i) for i in devices if i - distance in devices]
    return lax.ppermute(block, axis, route)


def on_device(
    queries, keys, values, outputs, out_grad, lse, sink_keys, sink_values, window_len, sink_live
):
    row_count = queries.shape[0]
    head_count = lse.shape[0]
    head_width = keys.shape[1]
    sink_count = sink_keys.shape[0]
    reach_count = WIN // row_count
    score_scale = head_width ** (-0.5)
    key_value = jnp.concatenate([keys, values], axis=1)
    received = []
    for distance in range(reach_count, 0, -1):
        received.append(shifted(key_value, ("seqhi", "seqlo"), distance))
    stacked = jnp.stack(received + [key_value])
    key_count = (reach_count + 1) * row_count
    key_block = stacked.reshape(key_count, 2 * head_width)
    key_part = key_block[:, :head_width]
    value_part = key_block[:, head_width:]
    device = lax.axis_index(("seqhi", "seqlo"))
    key_index = jnp.arange(key_count, dtype=jnp.int32)
    query_index = reach_count * row_count + jnp.arange(row_count, dtype=jnp.int32)
    distance_grid = query_index[:, None] - key_index[None, :]
    key_valid = key_index >= (reach_count - device) * row_count
    sink_index = jnp.arange(sink_count, dtype=jnp.int32)
    group_size = min(4, head_count)
    group_total = head_count // group_size
    query_heads = queries.reshape(row_count, head_count, head_width)
    out_heads = outputs.reshape(row_count, head_count, head_width)
    grad_heads = out_grad.reshape(row_count, head_count, head_width)

    def one_group(state_pair, group_id):
        pair_grad, sink_grad = state_pair
        begin = group_id * group_size
        query_group = lax.dynamic_slice_in_dim(query_heads, begin, group_size, 1)
        out_group = lax.dynamic_slice_in_dim(out_heads, begin, group_size, 1)
        grad_group = lax.dynamic_slice_in_dim(grad_heads, begin, group_size, 1)
        lse_group = lax.dynamic_slice_in_dim(lse, begin, group_size, 0)
        window_group = lax.dynamic_slice_in_dim(window_len, begin, group_size, 0)
        live_group = lax.dynamic_slice_in_dim(sink_live, begin, group_size, 0)
        inside = (
            (distance_grid >= 0)[None]
            & (distance_grid[None] < window_group[:, None, None])
            & key_valid[None, None, :]
        )
        scores = (
            jnp.einsum("tgd,kd->gtk", query_group, key_part, preferred_element_type=jnp.float32)
            * score_scale
        )
        probabilities = jnp.where(inside, jnp.exp(scores - lse_group[:, :, None]), 0.0)
        row_delta = jnp.sum(
            grad_group.astype(jnp.float32) * out_group.astype(jnp.float32), axis=2
        ).T
        dprobs = jnp.einsum(
            "tgd,kd->gtk", grad_group, value_part, preferred_element_type=jnp.float32
        )
        dscores = probabilities * (dprobs - row_delta[:, :, None])
        sink_inside = sink_index[None, None, :] < live_group[:, None, None]
        sink_scores = (
            jnp.einsum("tgd,sd->gts", query_group, sink_keys, preferred_element_type=jnp.float32)
            * score_scale
        )
        sink_probs = jnp.where(sink_inside, jnp.exp(sink_scores - lse_group[:, :, None]), 0.0)
        sink_dprobs = jnp.einsum(
            "tgd,sd->gts", grad_group, sink_values, preferred_element_type=jnp.float32
        )
        sink_dscores = sink_probs * (sink_dprobs - row_delta[:, :, None])
        probs_low = probabilities.astype(jnp.bfloat16)
        dscores_low = dscores.astype(jnp.bfloat16)
        sink_probs_low = sink_probs.astype(jnp.bfloat16)
        sink_ds_low = sink_dscores.astype(jnp.bfloat16)
        query_grad = (
            jnp.einsum("gtk,kd->tgd", dscores_low, key_part, preferred_element_type=jnp.float32)
            + jnp.einsum("gts,sd->tgd", sink_ds_low, sink_keys, preferred_element_type=jnp.float32)
        ) * score_scale
        key_grad = (
            jnp.einsum("gtk,tgd->kd", dscores_low, query_group, preferred_element_type=jnp.float32)
            * score_scale
        )
        value_grad = jnp.einsum(
            "gtk,tgd->kd", probs_low, grad_group, preferred_element_type=jnp.float32
        )
        sink_kgrad = (
            jnp.einsum("gts,tgd->sd", sink_ds_low, query_group, preferred_element_type=jnp.float32)
            * score_scale
        )
        sink_vgrad = jnp.einsum(
            "gts,tgd->sd", sink_probs_low, grad_group, preferred_element_type=jnp.float32
        )
        pair_grad = pair_grad + jnp.concatenate([key_grad, value_grad], axis=1)
        sink_grad = sink_grad + jnp.concatenate([sink_kgrad, sink_vgrad], axis=1)
        return ((pair_grad, sink_grad), query_grad)

    start_state = (
        jnp.zeros((key_count, 2 * head_width), jnp.float32),
        jnp.zeros((sink_count, 2 * head_width), jnp.float32),
    )
    (pair_grad, sink_grad), query_grads = lax.scan(
        one_group, start_state, jnp.arange(group_total, dtype=jnp.int32)
    )
    query_grad = query_grads.transpose(1, 0, 2, 3).reshape(row_count, head_count * head_width)
    by_offset = jnp.flip(pair_grad.reshape(reach_count + 1, row_count, 2 * head_width), axis=0)
    gathered_grad = by_offset[0]
    for distance in range(1, reach_count + 1):
        gathered_grad = gathered_grad + shifted(by_offset[distance], ("seqhi", "seqlo"), -distance)
    sink_total = lax.psum(sink_grad, ("seqhi", "seqlo"))
    return (
        query_grad,
        gathered_grad[:, :head_width],
        gathered_grad[:, head_width:],
        sink_total[:, :head_width],
        sink_total[:, head_width:],
    )


def solution(mesh):
    return jax.shard_map(
        on_device,
        mesh=mesh,
        in_specs=(
            P(("seqhi", "seqlo"), None),
            P(("seqhi", "seqlo"), None),
            P(("seqhi", "seqlo"), None),
            P(("seqhi", "seqlo"), None),
            P(("seqhi", "seqlo"), None),
            P(None, ("seqhi", "seqlo")),
            P(),
            P(),
            P(),
            P(),
        ),
        out_specs=(
            P(("seqhi", "seqlo"), None),
            P(("seqhi", "seqlo"), None),
            P(("seqhi", "seqlo"), None),
            P(),
            P(),
        ),
        check_vma=False,
    )
```

profile of v0, /device:TPU:32, one launch (start us, length us, event | category | flops | bytes accessed | tf_op | source)
XLA Modules:
  0.0 470.3 jit_solution(2523612800515310445)
XLA Ops:
  9.1 8.2 %collective-permute-start = (bf16[256,256]{1,0:T(8,128)(2,1)S(1)}, bf16[256,256]{1,0:T(8,128)(2,1)S(1)}, u32[]{:S(2)}, u32[]{:S(2)}) collective-permute-start(bf16[256,256]{1,0:T(8,128)(2,1)S(1)} %constant_dynamic-update-slice_fusion), channel_id=1, source_target_pairs={{0,8},{1,9},{2,10},{3,11},{4,12},{5,13},{6,14},{7,15},{8,16},{9,17... | collective-permute-start | bytes 393224 | tf_op jit(solution)/shard_map/ppermute | solution.py:12
  17.3 5.8 %collective-permute-start.1 = (bf16[256,256]{1,0:T(8,128)(2,1)S(1)}, bf16[256,256]{1,0:T(8,128)(2,1)S(1)}, u32[]{:S(2)}, u32[]{:S(2)}) collective-permute-start(bf16[256,256]{1,0:T(8,128)(2,1)S(1)} %constant_dynamic-update-slice_fusion), channel_id=1, source_target_pairs={{0,7},{1,8},{2,9},{3,10},{4,11},{5,12},{6,13},{7,14},{8,15},{9,16}... | collective-permute-start | bytes 393224 | tf_op jit(solution)/shard_map/ppermute | solution.py:12
  23.1 2.9 collective-permute-start.2
  26.0 5.6 %collective-permute-start.3 = (bf16[256,256]{1,0:T(8,128)(2,1)S(1)}, bf16[256,256]{1,0:T(8,128)(2,1)S(1)}, u32[]{:S(2)}, u32[]{:S(2)}) collective-permute-start(bf16[256,256]{1,0:T(8,128)(2,1)S(1)} %constant_dynamic-update-slice_fusion), channel_id=1, source_target_pairs={{0,5},{1,6},{2,7},{3,8},{4,9},{5,10},{6,11},{7,12},{8,13},{9,14},{... | collective-permute-start | bytes 393224 | tf_op jit(solution)/shard_map/ppermute | solution.py:12
  31.6 3.4 collective-permute-start.4
  35.0 2.3 copy.34
  40.0 3.8 collective-permute-start.5
  43.8 3.3 collective-permute-start.6
  47.2 2.5 collective-permute-start.7
  49.7 4.6 collective-permute-done.5
  54.3 7.2 %collective-permute-done.6 = bf16[256,256]{1,0:T(8,128)(2,1)S(1)} collective-permute-done((bf16[256,256]{1,0:T(8,128)(2,1)S(1)}, bf16[256,256]{1,0:T(8,128)(2,1)S(1)}, u32[]{:S(2)}, u32[]{:S(2)}) %collective-permute-start.6) | collective-permute-done | bytes 131104 | tf_op jit(solution)/shard_map/ppermute | solution.py:12
  61.5 3.6 collective-permute-done.7
  65.3 110.9 %while.16 = (s32[]{:T(128)}, f32[2304,256]{0,1:T(8,128)}, f32[128,256]{0,1:T(8,128)S(1)}, f32[4,256,4,128]{3,1,2,0:T(8,128)}, s32[4]{0:T(128)S(1)}, /*index=5*/s...) while((s32[]{:T(128)}, f32[2304,256]{0,1:T(8,128)}, ...), condition=%wide.region_2.3_spmd.clone.clone, body=%wide.region_0.2_spmd.clone.clone.sunk | while | flops 3216918272 | bytes 153292944 | solution.py:111
  69.2 5.1 %fusion.111 = f32[4,256,2304]{2,1,0:T(8,128)S(1)} fusion(f32[4,256]{1,0:T(4,128)S(1)} %constant_dynamic-slice_fusion.6, s32[256,2304]{1,0:T(8,128)S(1)} %iota_subtract_fusion.2, s32[4]{0:T(128)S(1)} %dynamic_slice.63, pred[2304]{0:T(1024)(128)(4,1)S(1)} %iota_compare_fusion.4, pred[256,2304]{1,0:T(8,128)(4,1)S(1)} %broadcast_compare_fusion.2, ...), kind=kOutput, calls=%fused_computation.8.clone.1 | convolution fusion | flops 618135552 | bytes 13244692 | tf_op jit(solution)/shard_map/while/body/eval_jaxpr/tgd,kd->gtk/dot_general | solution.py:60
  75.2 2.8 copy-done.1
  78.5 5.4 %fusion.113 = bf16[4,256,2304]{2,1,0:T(8,128)(2,1)S(1)} fusion(f32[4,256,2304]{2,1,0:T(8,128)} %copy-done.1, bf16[256,4,128]{0,2,1:T(8,128)(2,1)S(1)} %get-tuple-element.379, f32[4,256]{1,0:T(4,128)S(1)} %bitcast.152, bf16[2304,128]{1,0:T(8,128)(2,1)S(1)} %get-tuple-element.433), kind=kOutput, calls=%fused_computation.5.clone.1 | convolution fusion | flops 611057664 | bytes 15011840 | tf_op jit(solution)/shard_map/while/body/eval_jaxpr/tgd,kd->gtk/dot_general | solution.py:67
  84.0 2.0 fusion.114
  86.1 1.6 maximum_add_fusion.4
  96.2 5.1 %fusion.111 = f32[4,256,2304]{2,1,0:T(8,128)S(1)} fusion(f32[4,256]{1,0:T(4,128)S(1)} %constant_dynamic-slice_fusion.6, s32[256,2304]{1,0:T(8,128)S(1)} %iota_subtract_fusion.2, s32[4]{0:T(128)S(1)} %dynamic_slice.63, pred[2304]{0:T(1024)(128)(4,1)S(1)} %iota_compare_fusion.4, pred[256,2304]{1,0:T(8,128)(4,1)S(1)} %broadcast_compare_fusion.2, ...), kind=kOutput, calls=%fused_computation.8.clone.1 | convolution fusion | flops 618135552 | bytes 13244692 | tf_op jit(solution)/shard_map/while/body/eval_jaxpr/tgd,kd->gtk/dot_general | solution.py:60
  102.1 2.8 copy-done.1
  105.5 5.4 %fusion.113 = bf16[4,256,2304]{2,1,0:T(8,128)(2,1)S(1)} fusion(f32[4,256,2304]{2,1,0:T(8,128)} %copy-done.1, bf16[256,4,128]{0,2,1:T(8,128)(2,1)S(1)} %get-tuple-element.379, f32[4,256]{1,0:T(4,128)S(1)} %bitcast.152, bf16[2304,128]{1,0:T(8,128)(2,1)S(1)} %get-tuple-element.433), kind=kOutput, calls=%fused_computation.5.clone.1 | convolution fusion | flops 611057664 | bytes 15011840 | tf_op jit(solution)/shard_map/while/body/eval_jaxpr/tgd,kd->gtk/dot_general | solution.py:67
  110.9 2.0 fusion.114
  113.1 3.5 maximum_add_fusion.4
  124.1 5.1 %fusion.111 = f32[4,256,2304]{2,1,0:T(8,128)S(1)} fusion(f32[4,256]{1,0:T(4,128)S(1)} %constant_dynamic-slice_fusion.6, s32[256,2304]{1,0:T(8,128)S(1)} %iota_subtract_fusion.2, s32[4]{0:T(128)S(1)} %dynamic_slice.63, pred[2304]{0:T(1024)(128)(4,1)S(1)} %iota_compare_fusion.4, pred[256,2304]{1,0:T(8,128)(4,1)S(1)} %broadcast_compare_fusion.2, ...), kind=kOutput, calls=%fused_computation.8.clone.1 | convolution fusion | flops 618135552 | bytes 13244692 | tf_op jit(solution)/shard_map/while/body/eval_jaxpr/tgd,kd->gtk/dot_general | solution.py:60
  130.1 2.8 copy-done.1
  133.5 5.4 %fusion.113 = bf16[4,256,2304]{2,1,0:T(8,128)(2,1)S(1)} fusion(f32[4,256,2304]{2,1,0:T(8,128)} %copy-done.1, bf16[256,4,128]{0,2,1:T(8,128)(2,1)S(1)} %get-tuple-element.379, f32[4,256]{1,0:T(4,128)S(1)} %bitcast.152, bf16[2304,128]{1,0:T(8,128)(2,1)S(1)} %get-tuple-element.433), kind=kOutput, calls=%fused_computation.5.clone.1 | convolution fusion | flops 611057664 | bytes 15011840 | tf_op jit(solution)/shard_map/while/body/eval_jaxpr/tgd,kd->gtk/dot_general | solution.py:67
  138.9 2.0 fusion.114
  141.0 3.5 maximum_add_fusion.4
  152.1 5.1 %fusion.111 = f32[4,256,2304]{2,1,0:T(8,128)S(1)} fusion(f32[4,256]{1,0:T(4,128)S(1)} %constant_dynamic-slice_fusion.6, s32[256,2304]{1,0:T(8,128)S(1)} %iota_subtract_fusion.2, s32[4]{0:T(128)S(1)} %dynamic_slice.63, pred[2304]{0:T(1024)(128)(4,1)S(1)} %iota_compare_fusion.4, pred[256,2304]{1,0:T(8,128)(4,1)S(1)} %broadcast_compare_fusion.2, ...), kind=kOutput, calls=%fused_computation.8.clone.1 | convolution fusion | flops 618135552 | bytes 13244692 | tf_op jit(solution)/shard_map/while/body/eval_jaxpr/tgd,kd->gtk/dot_general | solution.py:60
  158.0 2.8 copy-done.1
  161.4 5.4 %fusion.113 = bf16[4,256,2304]{2,1,0:T(8,128)(2,1)S(1)} fusion(f32[4,256,2304]{2,1,0:T(8,128)} %copy-done.1, bf16[256,4,128]{0,2,1:T(8,128)(2,1)S(1)} %get-tuple-element.379, f32[4,256]{1,0:T(4,128)S(1)} %bitcast.152, bf16[2304,128]{1,0:T(8,128)(2,1)S(1)} %get-tuple-element.433), kind=kOutput, calls=%fused_computation.5.clone.1 | convolution fusion | flops 611057664 | bytes 15011840 | tf_op jit(solution)/shard_map/while/body/eval_jaxpr/tgd,kd->gtk/dot_general | solution.py:67
  166.9 2.0 fusion.114
  169.0 3.5 maximum_add_fusion.4
  176.2 2.0 copy.41
  179.4 3.8 collective-permute-start.15
  183.2 1.9 collective-permute-start.14
  185.1 4.4 collective-permute-start.13
  190.3 4.7 collective-permute-start.12
  194.9 5.9 %collective-permute-start.11 = (f32[256,256]{1,0:T(8,128)}, f32[256,256]{1,0:T(8,128)}, u32[]{:S(2)}, u32[]{:S(2)}) collective-permute-start(f32[256,256]{1,0:T(8,128)} %get-tuple-element.265), channel_id=1, source_target_pairs={{4,0},{5,1},{6,2},{7,3},{8,4},{9,5},{10,6},{11,7},{12,8},{13,9},{1... | collective-permute-start | bytes 786440 | tf_op jit(solution)/shard_map/ppermute | solution.py:12
  200.9 16.4 %collective-permute-done.15 = f32[256,256]{1,0:T(8,128)S(1)} collective-permute-done((f32[256,256]{1,0:T(8,128)}, f32[256,256]{1,0:T(8,128)S(1)}, u32[]{:S(2)}, u32[]{:S(2)}) %collective-permute-start.15) | collective-permute-done | bytes 262176 | tf_op jit(solution)/shard_map/ppermute | solution.py:12
  217.3 1.9 collective-permute-start.10
  219.2 4.6 collective-permute-done.14
  223.8 1.9 collective-permute-start.9
  227.0 1.9 collective-permute-start.8
  228.9 4.3 copy.40
  233.2 3.0 reshape.90
  236.2 223.5 %all-reduce.2.cloned.1.call-done = f32[128,256]{1,0:T(8,128)} async-done(((f32[128,256]{1,0:T(8,128)}), f32[128,256]{1,0:T(8,128)}) %all-reduce.2.cloned.1.call-update) | async-done | bytes 131088 | tf_op jit(solution)/shard_map/psum | solution.py:119
  459.7 1.5 fusion.53
  (200 shorter events, 44.7 us)
Async XLA Ops:
  7.2 30.2 %copy-start.7 = (bf16[256,2048]{1,0:T(8,128)(2,1)S(1)}, bf16[256,2048]{1,0:T(8,128)(2,1)}, u32[]{:S(2)}) copy-start(bf16[256,2048]{1,0:T(8,128)(2,1)} %param.16) | copy-start | bytes 3145732
  7.2 31.5 %copy-start.8 = (bf16[256,2048]{1,0:T(8,128)(2,1)S(1)}, bf16[256,2048]{1,0:T(8,128)(2,1)}, u32[]{:S(2)}) copy-start(bf16[256,2048]{1,0:T(8,128)(2,1)} %param.15) | copy-start | bytes 3145732
  7.2 452.5 %all-reduce.2.cloned.1.call-start = ((), (), s32[]{:S(2)}) async-start(), calls=%async_computation | async-start | bytes 262144 | tf_op jit(solution)/shard_map/psum | solution.py:119
  9.1 30.9 %collective-permute-start = (bf16[256,256]{1,0:T(8,128)(2,1)S(1)}, bf16[256,256]{1,0:T(8,128)(2,1)S(1)}, u32[]{:S(2)}, u32[]{:S(2)}) collective-permute-start(bf16[256,256]{1,0:T(8,128)(2,1)S(1)} %constant_dynamic-update-slice_fusion), channel_id=1, source_target_pairs={{0,8},{1,9},{2,10},{3,11},{4,12},{5,13},{6,14},{7,15},{8,16},{9,17... | collective-permute-start | bytes 393224 | tf_op jit(solution)/shard_map/ppermute | solution.py:12
  17.3 26.5 %collective-permute-start.1 = (bf16[256,256]{1,0:T(8,128)(2,1)S(1)}, bf16[256,256]{1,0:T(8,128)(2,1)S(1)}, u32[]{:S(2)}, u32[]{:S(2)}) collective-permute-start(bf16[256,256]{1,0:T(8,128)(2,1)S(1)} %constant_dynamic-update-slice_fusion), channel_id=1, source_target_pairs={{0,7},{1,8},{2,9},{3,10},{4,11},{5,12},{6,13},{7,14},{8,15},{9,16}... | collective-permute-start | bytes 393224 | tf_op jit(solution)/shard_map/ppermute | solution.py:12
  23.1 24.0 %collective-permute-start.2 = (bf16[256,256]{1,0:T(8,128)(2,1)S(1)}, bf16[256,256]{1,0:T(8,128)(2,1)S(1)}, u32[]{:S(2)}, u32[]{:S(2)}) collective-permute-start(bf16[256,256]{1,0:T(8,128)(2,1)S(1)} %constant_dynamic-update-slice_fusion), channel_id=1, source_target_pairs={{0,6},{1,7},{2,8},{3,9},{4,10},{5,11},{6,12},{7,13},{8,14},{9,15},... | collective-permute-start | bytes 393224 | tf_op jit(solution)/shard_map/ppermute | solution.py:12
  26.0 23.7 %collective-permute-start.3 = (bf16[256,256]{1,0:T(8,128)(2,1)S(1)}, bf16[256,256]{1,0:T(8,128)(2,1)S(1)}, u32[]{:S(2)}, u32[]{:S(2)}) collective-permute-start(bf16[256,256]{1,0:T(8,128)(2,1)S(1)} %constant_dynamic-update-slice_fusion), channel_id=1, source_target_pairs={{0,5},{1,6},{2,7},{3,8},{4,9},{5,10},{6,11},{7,12},{8,13},{9,14},{... | collective-permute-start | bytes 393224 | tf_op jit(solution)/shard_map/ppermute | solution.py:12
  31.6 18.1 %collective-permute-start.4 = (bf16[256,256]{1,0:T(8,128)(2,1)S(1)}, bf16[256,256]{1,0:T(8,128)(2,1)S(1)}, u32[]{:S(2)}, u32[]{:S(2)}) collective-permute-start(bf16[256,256]{1,0:T(8,128)(2,1)S(1)} %constant_dynamic-update-slice_fusion), channel_id=1, source_target_pairs={{0,4},{1,5},{2,6},{3,7},{4,8},{5,9},{6,10},{7,11},{8,12},{9,13},{1... | collective-permute-start | bytes 393224 | tf_op jit(solution)/shard_map/ppermute | solution.py:12
  40.0 25.3 %copy-start.9 = (bf16[128,128]{1,0:T(8,128)(2,1)S(1)}, bf16[128,128]{1,0:T(8,128)(2,1)}, u32[]{:S(2)}) copy-start(bf16[128,128]{1,0:T(8,128)(2,1)} %param.18) | copy-start | bytes 98308
  40.0 25.3 %copy-start.10 = (bf16[128,128]{1,0:T(8,128)(2,1)S(1)}, bf16[128,128]{1,0:T(8,128)(2,1)}, u32[]{:S(2)}) copy-start(bf16[128,128]{1,0:T(8,128)(2,1)} %param.19) | copy-start | bytes 98308
  40.0 25.3 %copy-start.11 = (s32[16]{0:T(128)S(1)}, s32[16]{0:T(128)}, u32[]{:S(2)}) copy-start(s32[16]{0:T(128)} %param.20) | copy-start | bytes 196
  40.0 25.3 %copy-start.12 = (s32[16]{0:T(128)S(1)}, s32[16]{0:T(128)}, u32[]{:S(2)}) copy-start(s32[16]{0:T(128)} %param.21) | copy-start | bytes 196
  40.0 14.3 %collective-permute-start.5 = (bf16[256,256]{1,0:T(8,128)(2,1)S(1)}, bf16[256,256]{1,0:T(8,128)(2,1)S(1)}, u32[]{:S(2)}, u32[]{:S(2)}) collective-permute-start(bf16[256,256]{1,0:T(8,128)(2,1)S(1)} %constant_dynamic-update-slice_fusion), channel_id=1, source_target_pairs={{0,3},{1,4},{2,5},{3,6},{4,7},{5,8},{6,9},{7,10},{8,11},{9,12},{10... | collective-permute-start | bytes 393224 | tf_op jit(solution)/shard_map/ppermute | solution.py:12
  43.8 17.7 %collective-permute-start.6 = (bf16[256,256]{1,0:T(8,128)(2,1)S(1)}, bf16[256,256]{1,0:T(8,128)(2,1)S(1)}, u32[]{:S(2)}, u32[]{:S(2)}) collective-permute-start(bf16[256,256]{1,0:T(8,128)(2,1)S(1)} %constant_dynamic-update-slice_fusion), channel_id=1, source_target_pairs={{0,2},{1,3},{2,4},{3,5},{4,6},{5,7},{6,8},{7,9},{8,10},{9,11},{10,... | collective-permute-start | bytes 393224 | tf_op jit(solution)/shard_map/ppermute | solution.py:12
  47.2 18.0 %collective-permute-start.7 = (bf16[256,256]{1,0:T(8,128)(2,1)S(1)}, bf16[256,256]{1,0:T(8,128)(2,1)S(1)}, u32[]{:S(2)}, u32[]{:S(2)}) collective-permute-start(bf16[256,256]{1,0:T(8,128)(2,1)S(1)} %constant_dynamic-update-slice_fusion), channel_id=1, source_target_pairs={{0,1},{1,2},{2,3},{3,4},{4,5},{5,6},{6,7},{7,8},{8,9},{9,10},{10,1... | collective-permute-start | bytes 393224 | tf_op jit(solution)/shard_map/ppermute | solution.py:12
  65.3 3.9 copy-start.4
  65.3 13.2 %copy-start.2 = (bf16[2304,128]{1,0:T(8,128)(2,1)}, bf16[2304,128]{1,0:T(8,128)(2,1)S(1)}, u32[]{:S(2)}) copy-start(bf16[2304,128]{1,0:T(8,128)(2,1)S(1)} %get-tuple-element.433) | copy-start | bytes 1769476 | tf_op jit(solution)/shard_map/while
  74.3 3.7 copy-start.1
  86.1 2.9 slice-start
  86.1 3.5 slice-start.1
  92.3 3.9 copy-start.4
  92.3 13.2 %copy-start.2 = (bf16[2304,128]{1,0:T(8,128)(2,1)}, bf16[2304,128]{1,0:T(8,128)(2,1)S(1)}, u32[]{:S(2)}) copy-start(bf16[2304,128]{1,0:T(8,128)(2,1)S(1)} %get-tuple-element.433) | copy-start | bytes 1769476 | tf_op jit(solution)/shard_map/while
  101.2 3.7 copy-start.1
  113.1 4.7 %slice-start = ((s8[4718592]{0:T(1024)(128)(4,1)}), s8[524288]{0:T(1024)(128)(4,1)S(1)}, s32[]{:S(2)}) async-start(s8[4718592]{0:T(1024)(128)(4,1)} %bitcast.145), calls=%async_computation.1 | async-start | bytes 1048576 | tf_op jit(solution)/shard_map/while
  113.1 3.6 copy-start.6
  113.1 4.8 %slice-start.1 = ((s8[4718592]{0:T(1024)(128)(4,1)}), s8[4194304]{0:T(1024)(128)(4,1)S(1)}, s32[]{:S(2)}) async-start(s8[4718592]{0:T(1024)(128)(4,1)} %bitcast.145), calls=%async_computation.2 | async-start | bytes 8388608 | tf_op jit(solution)/shard_map/while
  117.8 2.4 copy-start.3
  120.2 3.9 copy-start.4
  120.2 13.2 %copy-start.2 = (bf16[2304,128]{1,0:T(8,128)(2,1)}, bf16[2304,128]{1,0:T(8,128)(2,1)S(1)}, u32[]{:S(2)}) copy-start(bf16[2304,128]{1,0:T(8,128)(2,1)S(1)} %get-tuple-element.433) | copy-start | bytes 1769476 | tf_op jit(solution)/shard_map/while
  129.2 3.7 copy-start.1
  141.0 4.7 %slice-start = ((s8[4718592]{0:T(1024)(128)(4,1)}), s8[524288]{0:T(1024)(128)(4,1)S(1)}, s32[]{:S(2)}) async-start(s8[4718592]{0:T(1024)(128)(4,1)} %bitcast.145), calls=%async_computation.1 | async-start | bytes 1048576 | tf_op jit(solution)/shard_map/while
  141.0 3.6 copy-start.6
  141.0 4.8 %slice-start.1 = ((s8[4718592]{0:T(1024)(128)(4,1)}), s8[4194304]{0:T(1024)(128)(4,1)S(1)}, s32[]{:S(2)}) async-start(s8[4718592]{0:T(1024)(128)(4,1)} %bitcast.145), calls=%async_computation.2 | async-start | bytes 8388608 | tf_op jit(solution)/shard_map/while
  145.8 2.4 copy-start.3
  148.2 3.9 copy-start.4
  148.2 13.2 %copy-start.2 = (bf16[2304,128]{1,0:T(8,128)(2,1)}, bf16[2304,128]{1,0:T(8,128)(2,1)S(1)}, u32[]{:S(2)}) copy-start(bf16[2304,128]{1,0:T(8,128)(2,1)S(1)} %get-tuple-element.433) | copy-start | bytes 1769476 | tf_op jit(solution)/shard_map/while
  157.2 3.7 copy-start.1
  169.0 4.7 %slice-start = ((s8[4718592]{0:T(1024)(128)(4,1)}), s8[524288]{0:T(1024)(128)(4,1)S(1)}, s32[]{:S(2)}) async-start(s8[4718592]{0:T(1024)(128)(4,1)} %bitcast.145), calls=%async_computation.1 | async-start | bytes 1048576 | tf_op jit(solution)/shard_map/while
  169.0 3.6 copy-start.6
  169.0 4.8 %slice-start.1 = ((s8[4718592]{0:T(1024)(128)(4,1)}), s8[4194304]{0:T(1024)(128)(4,1)S(1)}, s32[]{:S(2)}) async-start(s8[4718592]{0:T(1024)(128)(4,1)} %bitcast.145), calls=%async_computation.2 | async-start | bytes 8388608 | tf_op jit(solution)/shard_map/while
  179.4 37.9 %collective-permute-start.15 = (f32[256,256]{1,0:T(8,128)}, f32[256,256]{1,0:T(8,128)S(1)}, u32[]{:S(2)}, u32[]{:S(2)}) collective-permute-start(f32[256,256]{1,0:T(8,128)} %get-tuple-element.261), channel_id=1, source_target_pairs={{8,0},{9,1},{10,2},{11,3},{12,4},{13,5},{14,6},{15,7},{16,8},{17,9... | collective-permute-start | bytes 786440 | tf_op jit(solution)/shard_map/ppermute | solution.py:12
  183.2 40.6 %collective-permute-start.14 = (f32[256,256]{1,0:T(8,128)}, f32[256,256]{1,0:T(8,128)S(1)}, u32[]{:S(2)}, u32[]{:S(2)}) collective-permute-start(f32[256,256]{1,0:T(8,128)} %get-tuple-element.262), channel_id=1, source_target_pairs={{7,0},{8,1},{9,2},{10,3},{11,4},{12,5},{13,6},{14,7},{15,8},{16,9}... | collective-permute-start | bytes 786440 | tf_op jit(solution)/shard_map/ppermute | solution.py:12
  185.1 41.8 %collective-permute-start.13 = (f32[256,256]{1,0:T(8,128)}, f32[256,256]{1,0:T(8,128)}, u32[]{:S(2)}, u32[]{:S(2)}) collective-permute-start(f32[256,256]{1,0:T(8,128)} %get-tuple-element.263), channel_id=1, source_target_pairs={{6,0},{7,1},{8,2},{9,3},{10,4},{11,5},{12,6},{13,7},{14,8},{15,9},... | collective-permute-start | bytes 786440 | tf_op jit(solution)/shard_map/ppermute | solution.py:12
  190.3 271.0 %collective-permute-start.12 = (f32[256,256]{1,0:T(8,128)}, f32[256,256]{1,0:T(8,128)}, u32[]{:S(2)}, u32[]{:S(2)}) collective-permute-start(f32[256,256]{1,0:T(8,128)} %get-tuple-element.264), channel_id=1, source_target_pairs={{5,0},{6,1},{7,2},{8,3},{9,4},{10,5},{11,6},{12,7},{13,8},{14,9},{... | collective-permute-start | bytes 786440 | tf_op jit(solution)/shard_map/ppermute | solution.py:12
  194.9 266.3 %collective-permute-start.11 = (f32[256,256]{1,0:T(8,128)}, f32[256,256]{1,0:T(8,128)}, u32[]{:S(2)}, u32[]{:S(2)}) collective-permute-start(f32[256,256]{1,0:T(8,128)} %get-tuple-element.265), channel_id=1, source_target_pairs={{4,0},{5,1},{6,2},{7,3},{8,4},{9,5},{10,6},{11,7},{12,8},{13,9},{1... | collective-permute-start | bytes 786440 | tf_op jit(solution)/shard_map/ppermute | solution.py:12
  217.3 243.9 %collective-permute-start.10 = (f32[256,256]{1,0:T(8,128)}, f32[256,256]{1,0:T(8,128)}, u32[]{:S(2)}, u32[]{:S(2)}) collective-permute-start(f32[256,256]{1,0:T(8,128)} %get-tuple-element.266), channel_id=1, source_target_pairs={{3,0},{4,1},{5,2},{6,3},{7,4},{8,5},{9,6},{10,7},{11,8},{12,9},{13... | collective-permute-start | bytes 786440 | tf_op jit(solution)/shard_map/ppermute | solution.py:12
  223.8 237.4 %collective-permute-start.9 = (f32[256,256]{1,0:T(8,128)S(1)}, f32[256,256]{1,0:T(8,128)}, u32[]{:S(2)}, u32[]{:S(2)}) collective-permute-start(f32[256,256]{1,0:T(8,128)S(1)} %get-tuple-element.267), channel_id=1, source_target_pairs={{2,0},{3,1},{4,2},{5,3},{6,4},{7,5},{8,6},{9,7},{10,8},{11,9},{12,... | collective-permute-start | bytes 786440 | tf_op jit(solution)/shard_map/ppermute | solution.py:12
  227.0 234.3 %collective-permute-start.8 = (f32[256,256]{1,0:T(8,128)S(1)}, f32[256,256]{1,0:T(8,128)}, u32[]{:S(2)}, u32[]{:S(2)}) collective-permute-start(f32[256,256]{1,0:T(8,128)S(1)} %get-tuple-element.260), channel_id=1, source_target_pairs={{1,0},{2,1},{3,2},{4,3},{5,4},{6,5},{7,6},{8,7},{9,8},{10,9},{11,1... | collective-permute-start | bytes 786440 | tf_op jit(solution)/shard_map/ppermute | solution.py:12
  (11 other events, 21.2 us)
Sparse Core Ops, SparseCore 0:
  190.4 269.2 all-reduce.1
where the time goes:
time: 474 us; the launch traced here: 470 us
  waiting for transfers between devices  261 us (55%)
  matrix products  67 us (14%)
  starting transfers between devices  61.9 us (13%)
  local copies, waits for them, and re-layouts  45.1 us (10%)
  other arithmetic  17.5 us (4%)
  between operations  14.4 us (3%)
    psum x1, waiting for transfers between devices, on_device(): sink_total = lax.psum(sink_grad, ('seqhi', 'seqlo'))  223 us
    ppermute x16, starting transfers between devices, shifted(): return lax.ppermute(block, axis, route)  61.8 us
    ppermute x16, waiting for transfers between devices, shifted(): return lax.ppermute(block, axis, route)  37.7 us
    dot_general x4, matrix products, one_group(): jnp.einsum('tgd,kd->gtk', grad_group, value_part, preferred_element_type=...  21.7 us
    dot_general x4, matrix products, one_group(): jnp.einsum('tgd,kd->gtk', query_group, key_part, preferred_element_type=j...  20.2 us
    while x72, local copies, waits for them, and re-layouts  12.8 us
    add x4, other arithmetic, one_group(): pair_grad = pair_grad + jnp.concatenate([key_grad, value_grad], axis=1)  12 us
  transfers between devices with their start and end apart: 17, of which 7 were waited for; matrix products, arithmetic and copies ran while one was open for 3% of the time, Pallas kernels for 0%

commit v1 on v0

v1 whole, which is shorter than its diff:
```python
import functools
import math

import jax
import jax.numpy as jnp
from jax import lax
from jax.experimental import pallas as pl
from jax.experimental.pallas import tpu as pltpu
from jax.sharding import PartitionSpec as P

MESH = pl.DeviceIdType.MESH
F32 = jnp.float32
BF16 = jnp.bfloat16
HI = 16
LO = 16
NDEV = HI * LO
COLS = 4
REACH = 8
TOK = 256
DH = 128
HEADS = 16
SCALE = DH ** (-0.5)
EXP2_SCALE = SCALE * math.log2(math.e)


def place(device):
    device = (device + NDEV) % NDEV
    return (device // LO, device % LO)


def whoami():
    hi, lo = lax.axis_index("seqhi"), lax.axis_index("seqlo")
    return hi, lo, hi * LO + lo


def greet(targets):
    barrier = pltpu.get_barrier_semaphore()
    for target in targets:
        pl.semaphore_signal(barrier, inc=1, device_id=target, device_id_type=MESH)
    pl.semaphore_wait(barrier, len(targets))


def gather_kernel(keys, values, out, local_sem, send_sem, recv_sem):
    _, _, me = whoami()
    col = me % COLS
    mates = [me - col + (col + j) % COLS for j in range(1, COLS)]
    cols = [(col + j) % COLS for j in range(1, COLS)]
    greet([place(me + COLS), place(me - COLS)] + [place(m) for m in mates])

    load_k = pltpu.make_async_copy(keys, out.at[REACH, 0], local_sem.at[0])
    load_v = pltpu.make_async_copy(values, out.at[REACH, 1], local_sem.at[1])
    load_k.start()
    load_v.start()
    load_k.wait()
    load_v.wait()

    def send(source, slot, target, index):
        return pltpu.make_async_remote_copy(
            src_ref=out.at[source],
            dst_ref=out.at[slot],
            send_sem=send_sem.at[index],
            recv_sem=recv_sem.at[slot],
            device_id=place(target),
            device_id_type=MESH,
        )

    send(REACH, 4, me + COLS, 0).start()
    for j in range(3):
        @pl.when(cols[j] > col)
        def _():
            send(REACH, REACH - (cols[j] - col), mates[j], 1 + j).start()
    send(4, 4, me + COLS, 0).wait_recv()
    send(4, 0, me + COLS, 4).start()
    for j in range(3):
        send(4, 4 - (cols[j] - col), mates[j], 5 + j).start()
    send(0, 0, me + COLS, 4).wait_recv()
    for j in range(3):
        @pl.when(cols[j] < col)
        def _():
            send(0, col - cols[j], mates[j], 1 + j).start()
    for slot in (1, 2, 3, 5, 6, 7):
        send(slot, slot, me + COLS, 0).wait_recv()
    for index in range(8):
        send(REACH, 4, me + COLS, index).wait_send()


def gather(keys, values):
    return pl.pallas_call(
        gather_kernel,
        out_shape=jax.ShapeDtypeStruct((REACH + 1, 2, TOK, DH), BF16),
        in_specs=[pl.BlockSpec(memory_space=pl.ANY)] * 2,
        out_specs=pl.BlockSpec(memory_space=pltpu.VMEM),
        scratch_shapes=[
            pltpu.SemaphoreType.DMA((2,)),
            pltpu.SemaphoreType.DMA((8,)),
            pltpu.SemaphoreType.DMA((REACH + 1,)),
        ],
        compiler_params=pltpu.CompilerParams(collective_id=0, has_side_effects=True),
        name="halo_gather",
    )(keys, values)


def nt_dot(a, b):
    return lax.dot_general(a, b, (((1,), (1,)), ((), ())), preferred_element_type=F32)


def dot(a, b):
    return jnp.dot(a, b, preferred_element_type=F32)


def split3(x):
    first = x.astype(BF16)
    rest = x - first.astype(F32)
    second = rest.astype(BF16)
    third = (rest - second.astype(F32)).astype(BF16)
    return first, second, third


def compute_kernel(
    window, live, q_ref, o_ref, g_ref, lse_ref, kv_ref, sk_ref, sv_ref,
    dq_ref, part_ref, own_ref, sink_ref, acc, dq_acc, lse_cols,
):
    head = pl.program_id(0)
    _, _, me = whoami()
    lane = lax.broadcasted_iota(jnp.int32, (TOK, DH), 1)

    @pl.when(head == 0)
    def _():
        acc[...] = jnp.zeros_like(acc)
        sink_ref[...] = jnp.zeros_like(sink_ref)
        pieces = jnp.concatenate(split3(lse_ref[...] * (-1.0 / SCALE)), axis=0)
        row = lax.broadcasted_iota(jnp.int32, (3 * HEADS, DH), 0)
        col = lax.broadcasted_iota(jnp.int32, (3 * HEADS, DH), 1)
        pick = (row == col).astype(BF16)
        lse_cols[...] = lax.dot_general(
            pieces, pick, (((0,), (0,)), ((), ())), preferred_element_type=F32
        )

    q = q_ref[...]
    g = g_ref[...]
    delta = jnp.sum(g.astype(F32) * o_ref[...].astype(F32), axis=1, keepdims=True)
    d1, d2, d3 = split3(-delta)
    minus_delta = jnp.where(
        lane == 0, d1.astype(F32), jnp.where(lane == 1, d2.astype(F32), jnp.where(lane == 2, d3.astype(F32), 0.0))
    ).astype(BF16)
    minus_lse = jnp.where(lane % HEADS == head, lse_cols[...], 0.0).astype(BF16)
    ones = jnp.ones((TOK, DH), BF16)
    q_aug = jnp.concatenate([q, minus_lse], axis=1)
    g_aug = jnp.concatenate([g, minus_delta], axis=1)
    q_t = q.T
    g_t = g.T

    span = window[head]
    s = nt_dot(q_aug, jnp.concatenate([sk_ref[...], ones[:DH]], axis=1))
    p = jnp.where(lane < live[head], jnp.exp2(s * EXP2_SCALE), 0.0)
    ds = p * nt_dot(g_aug, jnp.concatenate([sv_ref[...], ones[:DH]], axis=1))
    ds_low = ds.astype(BF16)
    dq_acc[...] = dot(ds_low, sk_ref[...])
    sink_ref[0] += dot(q_t, ds_low)
    sink_ref[1] += dot(g_t, p.astype(BF16))

    gap = lax.broadcasted_iota(jnp.int32, (TOK, TOK), 0) - lax.broadcasted_iota(jnp.int32, (TOK, TOK), 1)

    def block(back, masked):
        slot = REACH - back
        k = kv_ref[slot, 0]
        v = kv_ref[slot, 1]
        s = nt_dot(q_aug, jnp.concatenate([k, ones], axis=1))
        p = jnp.exp2(s * EXP2_SCALE)
        if masked:
            distance = gap + back * TOK
            p = jnp.where((distance >= 0) & (distance < span), p, 0.0)
        ds = p * nt_dot(g_aug, jnp.concatenate([v, ones], axis=1))
        ds_low = ds.astype(BF16)
        dq_acc[...] += dot(ds_low, k)
        acc[slot, 0] += dot(q_t, ds_low)
        acc[slot, 1] += dot(g_t, p.astype(BF16))

    block(0, True)
    full = jnp.minimum(span // TOK, me + 1)
    count = jnp.minimum((span + TOK - 2) // TOK, me) + 1

    def inner(back, carry):
        block(back, False)
        return carry

    def edge(back, carry):
        block(back, True)
        return carry

    lax.fori_loop(1, full, inner, 0)
    lax.fori_loop(jnp.maximum(full, 1), count, edge, 0)
    dq_ref[...] = dq_acc[...] * SCALE

    @pl.when(head == pl.num_programs(0) - 1)
    def _():
        sink_ref[0] = sink_ref[0] * SCALE
        for slot in range(REACH):
            part_ref[slot, 0] = (acc[slot, 0] * SCALE).astype(BF16)
            part_ref[slot, 1] = acc[slot, 1].astype(BF16)
        own_ref[0] = acc[REACH, 0] * SCALE
        own_ref[1] = acc[REACH, 1]


def compute(queries, outputs, out_grad, lse, key_value, sink_keys, sink_values, window_len, sink_live):
    by_head = pl.BlockSpec((TOK, DH), lambda h: (0, h))

    def whole(shape):
        return pl.BlockSpec(shape, lambda h: (0,) * len(shape))

    smem = pl.BlockSpec(memory_space=pltpu.SMEM)
    return pl.pallas_call(
        compute_kernel,
        grid=(HEADS,),
        out_shape=(
            jax.ShapeDtypeStruct((TOK, HEADS * DH), F32),
            jax.ShapeDtypeStruct((REACH, 2, DH, TOK), BF16),
            jax.ShapeDtypeStruct((2, DH, TOK), F32),
            jax.ShapeDtypeStruct((2, DH, DH), F32),
        ),
        in_specs=[
            smem, smem, by_head, by_head, by_head, whole((HEADS, TOK)),
            whole((REACH + 1, 2, TOK, DH)), whole((DH, DH)), whole((DH, DH)),
        ],
        out_specs=(
            by_head, whole((REACH, 2, DH, TOK)), whole((2, DH, TOK)), whole((2, DH, DH)),
        ),
        scratch_shapes=[
            pltpu.VMEM((REACH + 1, 2, DH, TOK), F32),
            pltpu.VMEM((TOK, DH), F32),
            pltpu.VMEM((TOK, DH), F32),
        ],
        compiler_params=pltpu.CompilerParams(dimension_semantics=("arbitrary",)),
        name="window_backward",
    )(window_len, sink_live, queries, outputs, out_grad, lse, key_value, sink_keys, sink_values)


def reduce_kernel(
    part, own, sink, dk, dv, sk_out, sv_out,
    from_mates, from_far, from_next, from_next_far, sum_near, sum_far, sink_in, sink_mid, sink_buf, sink_sum, sink_all,
    send_sem, recv_sem, s_send, s_recv,
):
    hi, lo, me = whoami()
    col = me % COLS
    mates = [me - col + (col + j) % COLS for j in range(1, COLS)]
    cols = [(col + j) % COLS for j in range(1, COLS)]
    piece = DH * 2 // LO

    barrier = pltpu.get_barrier_semaphore()
    for target in [place(me + COLS), place(me - COLS)]:
        pl.semaphore_signal(barrier, inc=1, device_id=target, device_id_type=MESH)

    def greet_group(i, carry):
        pl.semaphore_signal(barrier, inc=1, device_id=(hi, (lo + i) % LO), device_id_type=MESH)
        pl.semaphore_signal(barrier, inc=1, device_id=((hi + i) % HI, lo), device_id_type=MESH)
        return carry

    lax.fori_loop(1, LO, greet_group, 0)
    pl.semaphore_wait(barrier, 2 + 15 + 15)

    def exchange(phase, source, dest, along_lo):
        def copy(i):
            if along_lo:
                index = (lo + i) % LO
                mine, target = lo, (hi, index)
            else:
                index = (hi + i) % HI
                mine, target = hi, (index, lo)
            return pltpu.make_async_remote_copy(
                src_ref=source(index), dst_ref=dest(mine),
                send_sem=s_send.at[phase, i], recv_sem=s_recv.at[phase, mine],
                device_id=target, device_id_type=MESH,
            )

        def arrival(i):
            base = lo if along_lo else hi
            index = (base + i) % LO
            target = (hi, index) if along_lo else (index, lo)
            return pltpu.make_async_remote_copy(
                src_ref=source(index), dst_ref=dest(index),
                send_sem=s_send.at[phase, i], recv_sem=s_recv.at[phase, index],
                device_id=target, device_id_type=MESH,
            )

        def start():
            def body(i, carry):
                copy(i).start()
                return carry
            lax.fori_loop(1, LO, body, 0)

        def finish():
            def body(i, carry):
                arrival(i).wait_recv()
                copy(i).wait_send()
                return carry
            lax.fori_loop(1, LO, body, 0)

        return start, finish

    start1, finish1 = exchange(0, lambda i: sink.at[i], lambda i: sink_in.at[i], True)
    start2, finish2 = exchange(1, lambda i: sink_sum, lambda i: sink_mid.at[i], False)
    start3, finish3 = exchange(2, lambda i: sink_buf, lambda i: sink_all.at[i], True)

    def send(source, dest, target, index):
        return pltpu.make_async_remote_copy(
            src_ref=source, dst_ref=dest, send_sem=send_sem.at[index], recv_sem=recv_sem.at[index],
            device_id=place(target), device_id_type=MESH,
        )

    def mate_send(j, kind):
        to = 2 - j
        if kind == 0:
            return pltpu.make_async_remote_copy(
                src_ref=part.at[REACH - (4 + col - cols[j])], dst_ref=from_mates.at[to],
                send_sem=send_sem.at[j], recv_sem=recv_sem.at[to],
                device_id=place(mates[j]), device_id_type=MESH,
            )
        back = (col - cols[j] + REACH) % REACH
        return pltpu.make_async_remote_copy(
            src_ref=part.at[REACH - back], dst_ref=from_far.at[to],
            send_sem=send_sem.at[3 + j], recv_sem=recv_sem.at[3 + to],
            device_id=place(mates[j]), device_id_type=MESH,
        )

    def mate_arrival(j, kind):
        dest = from_mates if kind == 0 else from_far
        return pltpu.make_async_remote_copy(
            src_ref=part.at[0], dst_ref=dest.at[j], send_sem=send_sem.at[3 * kind + j],
            recv_sem=recv_sem.at[3 * kind + j], device_id=place(mates[j]), device_id_type=MESH,
        )

    start1()
    for j in range(3):
        mate_send(j, 1).start()
    for j in range(3):
        mate_send(j, 0).start()

    finish1()
    sink_in[lo] = sink[lo]
    total = sink_in[0]
    for i in range(1, LO):
        total = total + sink_in[i]
    sink_sum[...] = total
    start2()

    for j in range(3):
        mate_arrival(j, 1).wait_recv()
    for half in range(2):
        far = part[0, half].astype(F32)
        for j in range(3):
            far = far + jnp.where(cols[j] < col, from_far[j, half].astype(F32), 0.0)
        sum_far[half] = far.astype(BF16)
    far_send = send(sum_far, from_next_far, me - COLS, 6)
    far_send.start()

    finish2()
    sink_mid[hi] = sink_sum[...]
    total = sink_mid[0]
    for i in range(1, HI):
        total = total + sink_mid[i]
    sink_buf[...] = total
    start3()

    for j in range(3):
        mate_arrival(j, 0).wait_recv()
    far_send.wait_recv()
    for half in range(2):
        near = part[REACH - 4, half].astype(F32) + from_next_far[half].astype(F32)
        for j in range(3):
            near = near + from_mates[j, half].astype(F32)
        sum_near[half] = near.astype(BF16)
    near_send = send(sum_near, from_next, me - COLS, 7)
    near_send.start()

    finish3()
    sink_all[lo] = sink_buf[...]
    for i in range(LO // 2):
        sk_out[i * piece:(i + 1) * piece, :] = sink_all[i]
        sv_out[i * piece:(i + 1) * piece, :] = sink_all[LO // 2 + i]

    near_send.wait_recv()
    for half in range(2):
        total = own[half] + from_next[half].astype(F32)
        for j in range(3):
            total = total + jnp.where(cols[j] > col, from_far[j, half].astype(F32), 0.0)
        if half == 0:
            dk[...] = total.T
        else:
            dv[...] = total.T
    for j in range(3):
        mate_send(j, 0).wait_send()
        mate_send(j, 1).wait_send()
    far_send.wait_send()
    near_send.wait_send()


def reduce(part, own, sink):
    piece = DH * 2 // LO
    vmem = pl.BlockSpec(memory_space=pltpu.VMEM)
    block = (2, DH, TOK)
    return pl.pallas_call(
        reduce_kernel,
        out_shape=(
            jax.ShapeDtypeStruct((TOK, DH), F32),
            jax.ShapeDtypeStruct((TOK, DH), F32),
            jax.ShapeDtypeStruct((DH, DH), F32),
            jax.ShapeDtypeStruct((DH, DH), F32),
        ),
        in_specs=[vmem] * 3,
        out_specs=(vmem,) * 4,
        scratch_shapes=[
            pltpu.VMEM((3,) + block, BF16),
            pltpu.VMEM((3,) + block, BF16),
            pltpu.VMEM(block, BF16),
            pltpu.VMEM(block, BF16),
            pltpu.VMEM(block, BF16),
            pltpu.VMEM(block, BF16),
            pltpu.VMEM((LO, piece, DH), F32),
            pltpu.VMEM((HI, piece, DH), F32),
            pltpu.VMEM((piece, DH), F32),
            pltpu.VMEM((piece, DH), F32),
            pltpu.VMEM((LO, piece, DH), F32),
            pltpu.SemaphoreType.DMA((8,)),
            pltpu.SemaphoreType.DMA((8,)),
            pltpu.SemaphoreType.DMA((3, LO)),
            pltpu.SemaphoreType.DMA((3, LO)),
        ],
        compiler_params=pltpu.CompilerParams(collective_id=1, has_side_effects=True),
        name="gradient_reduce",
    )(part, own, sink.reshape(LO, piece, DH))


def on_device(
    queries, keys, values, outputs, out_grad, lse, sink_keys, sink_values, window_len, sink_live
):
    key_value = gather(keys, values)
    query_grad, part, own, sink = compute(
        queries, outputs, out_grad, lse, key_value, sink_keys, sink_values, window_len, sink_live
    )
    key_grad, value_grad, sk_t, sv_t = reduce(part, own, sink)
    return query_grad, key_grad, value_grad, sk_t.T, sv_t.T


def solution(mesh):
    rows = P(("seqhi", "seqlo"), None)
    return jax.shard_map(
        on_device,
        mesh=mesh,
        in_specs=(rows, rows, rows, rows, rows, P(None, ("seqhi", "seqlo")), P(), P(), P(), P()),
        out_specs=(rows, rows, rows, P(), P()),
        check_vma=False,
    )
```

time: 474 us -> 128 us (0.27)
  the two profiles are of different devices: /device:TPU:32 before, /device:TPU:24 now
where the time goes in v1:
time: 128 us; the launch traced here: 126 us
  Pallas kernels  119 us (93%)
  local copies, waits for them, and re-layouts  6.27 us (5%)
    pallas_call x1, Pallas kernels, reduce(): pl.pallas_call(reduce_kernel, out_shape=(jax.ShapeDtypeStruct((TOK, DH),...  54.6 us
    pallas_call x1, Pallas kernels, compute(): pl.pallas_call(compute_kernel, grid=(HEADS,), out_shape=(jax.ShapeDtypeSt...  36.5 us
    pallas_call x1, Pallas kernels, gather(): pl.pallas_call(gather_kernel, out_shape=jax.ShapeDtypeStruct((REACH + 1,...  27.9 us
    unnamed x4, local copies, waits for them, and re-layouts  6.27 us

profile of v1, /device:TPU:24, one launch (start us, length us, event | category | flops | bytes accessed | tf_op | source)
XLA Modules:
  0.0 126.0 jit_solution(13687446535729925963)
XLA Ops:
  0.6 27.9 %halo_gather.1.kv_ref = bf16[9,2,256,128]{3,2,1,0:T(8,128)(2,1)} custom-call(bf16[256,128]{1,0:T(8,128)(2,1)} %keys.1, bf16[256,128]{1,0:T(8,128)(2,1)} %values.1), custom_call_target="tpu_custom_call" | custom-call | tf_op jit(solution)/shard_map/halo_gather/pallas_call | solution.py:88
  28.6 36.5 %window_backward.1 = (f32[256,2048]{1,0:T(8,128)}, bf16[8,2,128,256]{3,2,1,0:T(8,128)(2,1)}, f32[2,128,256]{2,1,0:T(8,128)}, f32[2,128,128]{2,1,0:T(8,128)}) custom-call(s32[16]{0:T(128)} %window.1, s32[16]{0:T(128)} %live.1, bf16[256,2048]{1,0:T(8,128)(2,1)} %q_ref.1, bf16[256,2048]{1,0:T(8,128)(2,1)} %o_ref.1, bf16[256,2048]{1,0:T(8,128)(2,1)} %g_ref.1, ...), custom_call_target="tpu_custom_call" | custom-call | tf_op jit(solution)/shard_map/window_backward/pallas_call | solution.py:212
  65.1 54.6 %gradient_reduce.1 = (f32[256,128]{1,0:T(8,128)}, f32[256,128]{1,0:T(8,128)}, f32[128,128]{1,0:T(8,128)}, f32[128,128]{1,0:T(8,128)}) custom-call(bf16[8,2,128,256]{3,2,1,0:T(8,128)(2,1)} %get-tuple-element.14.part, f32[2,128,256]{2,1,0:T(8,128)} %get-tuple-element.15.own, f32[16,16,128]{2,1,0:T(8,128)} %bitcast.3), custom_call_target="tpu_custom_call" | custom-call | tf_op jit(solution)/shard_map/gradient_reduce/pallas_call | solution.py:401
  119.7 1.6 %copy.15 = f32[128,128]{1,0:T(8,128)} copy(f32[128,128]{0,1:T(8,128)} %bitcast.5) | data formatting | bytes 131072
  121.3 1.6 %copy.16 = f32[128,128]{1,0:T(8,128)} copy(f32[128,128]{0,1:T(8,128)} %bitcast.4) | data formatting | bytes 131072
  122.9 1.6 %copy.19 = f32[256,128]{1,0:T(8,128)} copy(f32[256,128]{1,0:T(8,128)} %get-tuple-element.32) | data formatting | bytes 262144
  124.5 1.6 %copy.20 = f32[256,128]{1,0:T(8,128)} copy(f32[256,128]{1,0:T(8,128)} %get-tuple-element.33) | data formatting | bytes 262144

commit v2 on v1

--- a/solution.py
+++ b/solution.py
@@ -16,6 +16,7 @@
 NDEV = HI * LO
 COLS = 4
 REACH = 8
+SINK_SLOT = REACH + 1
 TOK = 256
 DH = 128
 HEADS = 16
@@ -118,119 +119,164 @@
 
 def compute_kernel(
     window, live, q_ref, o_ref, g_ref, lse_ref, kv_ref, sk_ref, sv_ref,
-    dq_ref, part_ref, own_ref, sink_ref, acc, dq_acc, lse_cols,
+    dq_ref, part_ref, own_ref, sink_ref,
+    acc, dq_acc, q_aug, g_aug, q_t, g_t, k_aug, v_aug, gaps, lse_cols, ds_buf, p_buf, order, counts,
 ):
-    head = pl.program_id(0)
     _, _, me = whoami()
     lane = lax.broadcasted_iota(jnp.int32, (TOK, DH), 1)
-
-    @pl.when(head == 0)
-    def _():
-        acc[...] = jnp.zeros_like(acc)
-        sink_ref[...] = jnp.zeros_like(sink_ref)
-        pieces = jnp.concatenate(split3(lse_ref[...] * (-1.0 / SCALE)), axis=0)
-        row = lax.broadcasted_iota(jnp.int32, (3 * HEADS, DH), 0)
-        col = lax.broadcasted_iota(jnp.int32, (3 * HEADS, DH), 1)
-        pick = (row == col).astype(BF16)
-        lse_cols[...] = lax.dot_general(
-            pieces, pick, (((0,), (0,)), ((), ())), preferred_element_type=F32
-        )
-
-    q = q_ref[...]
-    g = g_ref[...]
-    delta = jnp.sum(g.astype(F32) * o_ref[...].astype(F32), axis=1, keepdims=True)
-    d1, d2, d3 = split3(-delta)
-    minus_delta = jnp.where(
-        lane == 0, d1.astype(F32), jnp.where(lane == 1, d2.astype(F32), jnp.where(lane == 2, d3.astype(F32), 0.0))
-    ).astype(BF16)
-    minus_lse = jnp.where(lane % HEADS == head, lse_cols[...], 0.0).astype(BF16)
+    pairs = HEADS // 2
+
+    for i in range(HEADS):
+        rank = 0
+        for j in range(HEADS):
+            if j != i:
+                before = window[j] <= window[i] if j < i else window[j] < window[i]
+                rank = rank + before.astype(jnp.int32)
+        order[rank] = i
+    total = pairs
+    for i in range(pairs):
+        longest = window[order[2 * i + 1]]
+        count = jnp.minimum((longest + TOK - 2) // TOK, me) + 1
+        counts[i] = count
+        total = total + count
+
+    acc[...] = jnp.zeros_like(acc)
+    dq_acc[...] = jnp.zeros_like(dq_acc)
     ones = jnp.ones((TOK, DH), BF16)
-    q_aug = jnp.concatenate([q, minus_lse], axis=1)
-    g_aug = jnp.concatenate([g, minus_delta], axis=1)
-    q_t = q.T
-    g_t = g.T
-
-    span = window[head]
-    s = nt_dot(q_aug, jnp.concatenate([sk_ref[...], ones[:DH]], axis=1))
-    p = jnp.where(lane < live[head], jnp.exp2(s * EXP2_SCALE), 0.0)
-    ds = p * nt_dot(g_aug, jnp.concatenate([sv_ref[...], ones[:DH]], axis=1))
-    ds_low = ds.astype(BF16)
-    dq_acc[...] = dot(ds_low, sk_ref[...])
-    sink_ref[0] += dot(q_t, ds_low)
-    sink_ref[1] += dot(g_t, p.astype(BF16))
-
-    gap = lax.broadcasted_iota(jnp.int32, (TOK, TOK), 0) - lax.broadcasted_iota(jnp.int32, (TOK, TOK), 1)
-
-    def block(back, masked):
-        slot = REACH - back
-        k = kv_ref[slot, 0]
-        v = kv_ref[slot, 1]
-        s = nt_dot(q_aug, jnp.concatenate([k, ones], axis=1))
+    for slot in range(REACH + 1):
+        k_aug[slot, :, :DH] = kv_ref[slot, 0]
+        v_aug[slot, :, :DH] = kv_ref[slot, 1]
+        k_aug[slot, :, DH:] = ones
+        v_aug[slot, :, DH:] = ones
+    zeros = jnp.zeros((TOK, 2 * DH), BF16)
+    k_aug[SINK_SLOT] = zeros
+    v_aug[SINK_SLOT] = zeros
+    k_aug[SINK_SLOT, :DH, :DH] = sk_ref[...]
+    v_aug[SINK_SLOT, :DH, :DH] = sv_ref[...]
+    k_aug[SINK_SLOT, :DH, DH:] = ones[:DH]
+    v_aug[SINK_SLOT, :DH, DH:] = ones[:DH]
+    row_at = lax.broadcasted_iota(jnp.int32, (TOK, TOK), 0)
+    col_at = lax.broadcasted_iota(jnp.int32, (TOK, TOK), 1)
+    gaps[0] = row_at - col_at
+    gaps[1] = col_at - row_at
+    gaps[2] = col_at
+
+    pieces = jnp.concatenate(split3(lse_ref[...] * (-1.0 / SCALE)), axis=0)
+    row = lax.broadcasted_iota(jnp.int32, (3 * HEADS, DH), 0)
+    col = lax.broadcasted_iota(jnp.int32, (3 * HEADS, DH), 1)
+    pick = (row == col).astype(BF16)
+    lse_cols[...] = lax.dot_general(
+        pieces, pick, (((0,), (0,)), ((), ())), preferred_element_type=F32
+    )
+
+    def prepare(head, carry):
+        at = pl.ds(pl.multiple_of(head * DH, DH), DH)
+        q = q_ref[:, at]
+        g = g_ref[:, at]
+        delta = jnp.sum(g.astype(F32) * o_ref[:, at].astype(F32), axis=1, keepdims=True)
+        d1, d2, d3 = split3(-delta)
+        minus_delta = jnp.where(
+            lane == 0, d1.astype(F32),
+            jnp.where(lane == 1, d2.astype(F32), jnp.where(lane == 2, d3.astype(F32), 0.0)),
+        ).astype(BF16)
+        minus_lse = jnp.where(lane % HEADS == head, lse_cols[...], 0.0).astype(BF16)
+        q_aug[head, :, :DH] = q
+        q_aug[head, :, DH:] = minus_lse
+        g_aug[head, :, :DH] = g
+        g_aug[head, :, DH:] = minus_delta
+        q_t[head] = q.T
+        g_t[head] = g.T
+        return carry
+
+    lax.fori_loop(0, HEADS, prepare, 0)
+
+    def scores(pair, back, dead):
+        sink = back < 0
+        slot = jnp.where(sink, SINK_SLOT, REACH - back)
+        kind = jnp.where(sink, 2, jnp.where(back == 0, 1, 0))
+        first, second = order[2 * pair], order[2 * pair + 1]
+
+        def threshold(head):
+            inside = jnp.where(back == 0, 1, window[head] - back * TOK)
+            return jnp.where(dead, -(1 << 20), jnp.where(sink, live[head], inside))
+
+        q = jnp.concatenate([q_aug[first], q_aug[second]], axis=0)
+        g = jnp.concatenate([g_aug[first], g_aug[second]], axis=0)
+        s = nt_dot(q, k_aug[slot])
+        dp = nt_dot(g, v_aug[slot])
         p = jnp.exp2(s * EXP2_SCALE)
-        if masked:
-            distance = gap + back * TOK
-            p = jnp.where((distance >= 0) & (distance < span), p, 0.0)
-        ds = p * nt_dot(g_aug, jnp.concatenate([v, ones], axis=1))
-        ds_low = ds.astype(BF16)
-        dq_acc[...] += dot(ds_low, k)
-        acc[slot, 0] += dot(q_t, ds_low)
-        acc[slot, 1] += dot(g_t, p.astype(BF16))
-
-    block(0, True)
-    full = jnp.minimum(span // TOK, me + 1)
-    count = jnp.minimum((span + TOK - 2) // TOK, me) + 1
-
-    def inner(back, carry):
-        block(back, False)
-        return carry
-
-    def edge(back, carry):
-        block(back, True)
-        return carry
-
-    lax.fori_loop(1, full, inner, 0)
-    lax.fori_loop(jnp.maximum(full, 1), count, edge, 0)
-    dq_ref[...] = dq_acc[...] * SCALE
-
-    @pl.when(head == pl.num_programs(0) - 1)
-    def _():
-        sink_ref[0] = sink_ref[0] * SCALE
-        for slot in range(REACH):
-            part_ref[slot, 0] = (acc[slot, 0] * SCALE).astype(BF16)
-            part_ref[slot, 1] = acc[slot, 1].astype(BF16)
-        own_ref[0] = acc[REACH, 0] * SCALE
-        own_ref[1] = acc[REACH, 1]
+        gap = gaps[kind]
+        inside = jnp.concatenate([gap < threshold(first), gap < threshold(second)], axis=0)
+        p = jnp.where(inside, p, 0.0)
+        ds_buf[...] = (p * dp).astype(BF16)
+        p_buf[...] = p.astype(BF16)
+
+    def gradients(pair, back):
+        slot = jnp.where(back < 0, SINK_SLOT, REACH - back)
+        first, second = order[2 * pair], order[2 * pair + 1]
+        ds = ds_buf[...]
+        p = p_buf[...]
+        dq = dot(ds, k_aug[slot, :, :DH])
+        dk = dot(jnp.concatenate([q_t[first], q_t[second]], axis=1), ds)
+        dv = dot(jnp.concatenate([g_t[first], g_t[second]], axis=1), p)
+        dq_acc[first] += dq[:TOK]
+        dq_acc[second] += dq[TOK:]
+        acc[slot, 0] += dk
+        acc[slot, 1] += dv
+
+    scores(0, -1, False)
+
+    def step(i, item):
+        pair, back = item
+        last = back + 1 >= counts[pair]
+        next_pair = jnp.minimum(jnp.where(last, pair + 1, pair), pairs - 1)
+        next_back = jnp.where(last, -1, back + 1)
+        gradients(pair, back)
+        scores(next_pair, next_back, i + 1 >= total)
+        return next_pair, next_back
+
+    lax.fori_loop(0, total, step, (0, -1))
+
+    for head in range(HEADS):
+        dq_ref[:, head * DH:(head + 1) * DH] = dq_acc[head] * SCALE
+    sink_ref[0] = acc[SINK_SLOT, 0, :, :DH] * SCALE
+    sink_ref[1] = acc[SINK_SLOT, 1, :, :DH]
+    for slot in range(REACH):
+        part_ref[slot, 0] = (acc[slot, 0] * SCALE).astype(BF16)
+        part_ref[slot, 1] = acc[slot, 1].astype(BF16)
+    own_ref[0] = acc[REACH, 0] * SCALE
+    own_ref[1] = acc[REACH, 1]
 
 
 def compute(queries, outputs, out_grad, lse, key_value, sink_keys, sink_values, window_len, sink_live):
-    by_head = pl.BlockSpec((TOK, DH), lambda h: (0, h))
-
-    def whole(shape):
-        return pl.BlockSpec(shape, lambda h: (0,) * len(shape))
-
     smem = pl.BlockSpec(memory_space=pltpu.SMEM)
+    vmem = pl.BlockSpec(memory_space=pltpu.VMEM)
     return pl.pallas_call(
         compute_kernel,
-        grid=(HEADS,),
         out_shape=(
             jax.ShapeDtypeStruct((TOK, HEADS * DH), F32),
             jax.ShapeDtypeStruct((REACH, 2, DH, TOK), BF16),
             jax.ShapeDtypeStruct((2, DH, TOK), F32),
             jax.ShapeDtypeStruct((2, DH, DH), F32),
         ),
-        in_specs=[
-            smem, smem, by_head, by_head, by_head, whole((HEADS, TOK)),
-            whole((REACH + 1, 2, TOK, DH)), whole((DH, DH)), whole((DH, DH)),
+        in_specs=[smem] * 2 + [vmem] * 7,
+        out_specs=(vmem,) * 4,
+        scratch_shapes=[
+            pltpu.VMEM((SINK_SLOT + 1, 2, DH, TOK), F32),
+            pltpu.VMEM((HEADS, TOK, DH), F32),
+            pltpu.VMEM((HEADS, TOK, 2 * DH), BF16),
+            pltpu.VMEM((HEADS, TOK, 2 * DH), BF16),
+            pltpu.VMEM((HEADS, DH, TOK), BF16),
+            pltpu.VMEM((HEADS, DH, TOK), BF16),
+            pltpu.VMEM((SINK_SLOT + 1, TOK, 2 * DH), BF16),
+            pltpu.VMEM((SINK_SLOT + 1, TOK, 2 * DH), BF16),
+            pltpu.VMEM((3, TOK, TOK), jnp.int32),
+            pltpu.VMEM((TOK, DH), F32),
+            pltpu.VMEM((2 * TOK, TOK), BF16),
+            pltpu.VMEM((2 * TOK, TOK), BF16),
+            pltpu.SMEM((HEADS,), jnp.int32),
+            pltpu.SMEM((HEADS // 2,), jnp.int32),
         ],
-        out_specs=(
-            by_head, whole((REACH, 2, DH, TOK)), whole((2, DH, TOK)), whole((2, DH, DH)),
-        ),
-        scratch_shapes=[
-            pltpu.VMEM((REACH + 1, 2, DH, TOK), F32),
-            pltpu.VMEM((TOK, DH), F32),
-            pltpu.VMEM((TOK, DH), F32),
-        ],
-        compiler_params=pltpu.CompilerParams(dimension_semantics=("arbitrary",)),
         name="window_backward",
     )(window_len, sink_live, queries, outputs, out_grad, lse, key_value, sink_keys, sink_values)
 

time: 128 us -> 110 us (0.86)
  the two profiles are of different devices: /device:TPU:24 before, /device:TPU:32 now
where the time goes in v2:
time: 110 us; the launch traced here: 111 us
  Pallas kernels  104 us (95%)
  local copies, waits for them, and re-layouts  6.27 us (6%)
    pallas_call x1, Pallas kernels, compute(): pl.pallas_call(compute_kernel, out_shape=(jax.ShapeDtypeStruct((TOK, HEAD...  39.3 us
    pallas_call x1, Pallas kernels, reduce(): pl.pallas_call(reduce_kernel, out_shape=(jax.ShapeDtypeStruct((TOK, DH),...  37.1 us
    pallas_call x1, Pallas kernels, gather(): pl.pallas_call(gather_kernel, out_shape=jax.ShapeDtypeStruct((REACH + 1,...  27.9 us
    unnamed x4, local copies, waits for them, and re-layouts  6.27 us

profile of v2, /device:TPU:32, one launch (start us, length us, event | category | flops | bytes accessed | tf_op | source)
XLA Modules:
  0.0 111.2 jit_solution(12740932694389446445)
XLA Ops:
  0.6 27.9 %halo_gather.1.kv_ref = bf16[9,2,256,128]{3,2,1,0:T(8,128)(2,1)} custom-call(bf16[256,128]{1,0:T(8,128)(2,1)} %keys.1, bf16[256,128]{1,0:T(8,128)(2,1)} %values.1), custom_call_target="tpu_custom_call" | custom-call | tf_op jit(solution)/shard_map/halo_gather/pallas_call | solution.py:89
  28.6 39.3 %window_backward.1 = (f32[256,2048]{1,0:T(8,128)}, bf16[8,2,128,256]{3,2,1,0:T(8,128)(2,1)}, f32[2,128,256]{2,1,0:T(8,128)}, f32[2,128,128]{2,1,0:T(8,128)}) custom-call(s32[16]{0:T(128)} %window.1, s32[16]{0:T(128)} %live.1, bf16[256,2048]{1,0:T(8,128)(2,1)} %q_ref.1, bf16[256,2048]{1,0:T(8,128)(2,1)} %o_ref.1, bf16[256,2048]{1,0:T(8,128)(2,1)} %g_ref.1, ...), custom_call_target="tpu_custom_call" | custom-call | tf_op jit(solution)/shard_map/window_backward/pallas_call | solution.py:254
  67.9 37.1 %gradient_reduce.1 = (f32[256,128]{1,0:T(8,128)}, f32[256,128]{1,0:T(8,128)}, f32[128,128]{1,0:T(8,128)}, f32[128,128]{1,0:T(8,128)}) custom-call(bf16[8,2,128,256]{3,2,1,0:T(8,128)(2,1)} %get-tuple-element.14.part, f32[2,128,256]{2,1,0:T(8,128)} %get-tuple-element.15.own, f32[16,16,128]{2,1,0:T(8,128)} %bitcast.3), custom_call_target="tpu_custom_call" | custom-call | tf_op jit(solution)/shard_map/gradient_reduce/pallas_call | solution.py:447
  104.9 1.6 %copy.15 = f32[128,128]{1,0:T(8,128)} copy(f32[128,128]{0,1:T(8,128)} %bitcast.5) | data formatting | bytes 131072
  106.5 1.6 %copy.16 = f32[128,128]{1,0:T(8,128)} copy(f32[128,128]{0,1:T(8,128)} %bitcast.4) | data formatting | bytes 131072
  108.1 1.6 %copy.19 = f32[256,128]{1,0:T(8,128)} copy(f32[256,128]{1,0:T(8,128)} %get-tuple-element.32) | data formatting | bytes 262144
  109.6 1.6 %copy.20 = f32[256,128]{1,0:T(8,128)} copy(f32[256,128]{1,0:T(8,128)} %get-tuple-element.33) | data formatting | bytes 262144

commit v3 on v2

--- a/solution.py
+++ b/solution.py
@@ -46,7 +46,7 @@
     col = me % COLS
     mates = [me - col + (col + j) % COLS for j in range(1, COLS)]
     cols = [(col + j) % COLS for j in range(1, COLS)]
-    greet([place(me + COLS), place(me - COLS)] + [place(m) for m in mates])
+    greet([place(me + d) for d in (COLS, -COLS)] + [place(m) for m in mates])
 
     load_k = pltpu.make_async_copy(keys, out.at[REACH, 0], local_sem.at[0])
     load_v = pltpu.make_async_copy(values, out.at[REACH, 1], local_sem.at[1])
@@ -120,7 +120,7 @@
 def compute_kernel(
     window, live, q_ref, o_ref, g_ref, lse_ref, kv_ref, sk_ref, sv_ref,
     dq_ref, part_ref, own_ref, sink_ref,
-    acc, dq_acc, q_aug, g_aug, q_t, g_t, k_aug, v_aug, gaps, lse_cols, ds_buf, p_buf, order, counts,
+    acc, dq_acc, q_aug, g_aug, q_t, g_t, k_aug, v_aug, gaps, lse_cols, ds_a, p_a, ds_b, p_b, order, counts,
 ):
     _, _, me = whoami()
     lane = lax.broadcasted_iota(jnp.int32, (TOK, DH), 1)
@@ -190,7 +190,8 @@
 
     lax.fori_loop(0, HEADS, prepare, 0)
 
-    def scores(pair, back, dead):
+    def scores(item, dead, ds_buf, p_buf):
+        pair, back = item
         sink = back < 0
         slot = jnp.where(sink, SINK_SLOT, REACH - back)
         kind = jnp.where(sink, 2, jnp.where(back == 0, 1, 0))
@@ -211,7 +212,8 @@
         ds_buf[...] = (p * dp).astype(BF16)
         p_buf[...] = p.astype(BF16)
 
-    def gradients(pair, back):
+    def gradients(item, ds_buf, p_buf):
+        pair, back = item
         slot = jnp.where(back < 0, SINK_SLOT, REACH - back)
         first, second = order[2 * pair], order[2 * pair + 1]
         ds = ds_buf[...]
@@ -224,18 +226,23 @@
         acc[slot, 0] += dk
         acc[slot, 1] += dv
 
-    scores(0, -1, False)
-
-    def step(i, item):
+    def advance(item):
         pair, back = item
         last = back + 1 >= counts[pair]
-        next_pair = jnp.minimum(jnp.where(last, pair + 1, pair), pairs - 1)
-        next_back = jnp.where(last, -1, back + 1)
-        gradients(pair, back)
-        scores(next_pair, next_back, i + 1 >= total)
-        return next_pair, next_back
-
-    lax.fori_loop(0, total, step, (0, -1))
+        return jnp.minimum(jnp.where(last, pair + 1, pair), pairs - 1), jnp.where(last, -1, back + 1)
+
+    scores((0, -1), False, ds_a, p_a)
+
+    def step(i, item):
+        second = advance(item)
+        third = advance(second)
+        scores(second, 2 * i + 1 >= total, ds_b, p_b)
+        gradients(item, ds_a, p_a)
+        scores(third, 2 * i + 2 >= total, ds_a, p_a)
+        gradients(second, ds_b, p_b)
+        return third
+
+    lax.fori_loop(0, (total + 1) // 2, step, (0, -1))
 
     for head in range(HEADS):
         dq_ref[:, head * DH:(head + 1) * DH] = dq_acc[head] * SCALE
@@ -274,6 +281,8 @@
             pltpu.VMEM((TOK, DH), F32),
             pltpu.VMEM((2 * TOK, TOK), BF16),
             pltpu.VMEM((2 * TOK, TOK), BF16),
+            pltpu.VMEM((2 * TOK, TOK), BF16),
+            pltpu.VMEM((2 * TOK, TOK), BF16),
             pltpu.SMEM((HEADS,), jnp.int32),
             pltpu.SMEM((HEADS // 2,), jnp.int32),
         ],
@@ -293,7 +302,7 @@
     piece = DH * 2 // LO
 
     barrier = pltpu.get_barrier_semaphore()
-    for target in [place(me + COLS), place(me - COLS)]:
+    for target in [place(me + d) for d in (COLS, -COLS)]:
         pl.semaphore_signal(barrier, inc=1, device_id=target, device_id_type=MESH)
 
     def greet_group(i, carry):
@@ -476,6 +485,24 @@
     )(part, own, sink.reshape(LO, piece, DH))
 
 
+def finish_kernel(dk, dv, sk_t, sv_t, dk_out, dv_out, sk_out, sv_out):
+    dk_out[...] = dk[...]
+    dv_out[...] = dv[...]
+    sk_out[...] = sk_t[...].T
+    sv_out[...] = sv_t[...].T
+
+
+def finish(dk, dv, sk_t, sv_t):
+    vmem = pl.BlockSpec(memory_space=pltpu.VMEM)
+    return pl.pallas_call(
+        finish_kernel,
+        out_shape=[jax.ShapeDtypeStruct(x.shape, F32) for x in (dk, dv, sk_t, sv_t)],
+        in_specs=[vmem] * 4,
+        out_specs=[vmem] * 4,
+        name="finish",
+    )(dk, dv, sk_t, sv_t)
+
+
 def on_device(
     queries, keys, values, outputs, out_grad, lse, sink_keys, sink_values, window_len, sink_live
 ):
@@ -484,7 +511,7 @@
         queries, outputs, out_grad, lse, key_value, sink_keys, sink_values, window_len, sink_live
     )
     key_grad, value_grad, sk_t, sv_t = reduce(part, own, sink)
-    return query_grad, key_grad, value_grad, sk_t.T, sv_t.T
+    return (query_grad,) + tuple(finish(key_grad, value_grad, sk_t, sv_t))
 
 
 def solution(mesh):

time: 110 us -> 101 us (0.918); the launches traced: 111 us -> 98.7 us
  local copies, waits for them, and re-layouts: 6.27 us -> 0 us
  Pallas kernels: 104 us -> 98 us
    pallas_call x1, Pallas kernels: 39.3 us -> 31.2 us  [compute(): pl.pallas_call(compute_kernel, out_shape=(jax.ShapeDtypeStruct((TOK, HEAD...]
    unnamed x4 -> x0, local copies, waits for them, and re-layouts: 6.27 us -> none
    pallas_call x0 -> x1, Pallas kernels: none -> 1.75 us  [finish(): pl.pallas_call(finish_kernel, out_shape=[jax.ShapeDtypeStruct(x.shape, F3...]
where the time goes in v3:
time: 101 us; the launch traced here: 98.7 us
  Pallas kernels  98 us (97%)
    pallas_call x1, Pallas kernels, reduce(): pl.pallas_call(reduce_kernel, out_shape=(jax.ShapeDtypeStruct((TOK, DH),...  37.1 us
    pallas_call x1, Pallas kernels, compute(): pl.pallas_call(compute_kernel, out_shape=(jax.ShapeDtypeStruct((TOK, HEAD...  31.2 us
    pallas_call x1, Pallas kernels, gather(): pl.pallas_call(gather_kernel, out_shape=jax.ShapeDtypeStruct((REACH + 1,...  27.9 us

profile of v3, /device:TPU:32, one launch (start us, length us, event | category | flops | bytes accessed | tf_op | source)
XLA Modules:
  0.0 98.7 jit_solution(14367471789708302474)
XLA Ops:
  0.6 27.9 %halo_gather.1.kv_ref = bf16[9,2,256,128]{3,2,1,0:T(8,128)(2,1)} custom-call(bf16[256,128]{1,0:T(8,128)(2,1)} %keys.1, bf16[256,128]{1,0:T(8,128)(2,1)} %values.1), custom_call_target="tpu_custom_call" | custom-call | tf_op jit(solution)/shard_map/halo_gather/pallas_call | solution.py:89
  28.6 31.2 %window_backward.1 = (f32[256,2048]{1,0:T(8,128)}, bf16[8,2,128,256]{3,2,1,0:T(8,128)(2,1)}, f32[2,128,256]{2,1,0:T(8,128)}, f32[2,128,128]{2,1,0:T(8,128)}) custom-call(s32[16]{0:T(128)} %window.1, s32[16]{0:T(128)} %live.1, bf16[256,2048]{1,0:T(8,128)(2,1)} %q_ref.1, bf16[256,2048]{1,0:T(8,128)(2,1)} %o_ref.1, bf16[256,2048]{1,0:T(8,128)(2,1)} %g_ref.1, ...), custom_call_target="tpu_custom_call" | custom-call | tf_op jit(solution)/shard_map/window_backward/pallas_call | solution.py:261
  59.8 37.1 %gradient_reduce.1 = (f32[256,128]{1,0:T(8,128)}, f32[256,128]{1,0:T(8,128)}, f32[128,128]{1,0:T(8,128)}, f32[128,128]{1,0:T(8,128)}) custom-call(bf16[8,2,128,256]{3,2,1,0:T(8,128)(2,1)} %get-tuple-element.18.part, f32[2,128,256]{2,1,0:T(8,128)} %get-tuple-element.19.own, f32[16,16,128]{2,1,0:T(8,128)} %bitcast.1), custom_call_target="tpu_custom_call" | custom-call | tf_op jit(solution)/shard_map/gradient_reduce/pallas_call | solution.py:456
  96.9 1.8 %finish.1 = (f32[256,128]{1,0:T(8,128)}, f32[256,128]{1,0:T(8,128)}, f32[128,128]{1,0:T(8,128)}, f32[128,128]{1,0:T(8,128)}) custom-call(f32[256,128]{1,0:T(8,128)} %get-tuple-element.21.dk, f32[256,128]{1,0:T(8,128)} %get-tuple-element.22.dv, f32[128,128]{1,0:T(8,128)} %get-tuple-element.23.sk_t, f32[128,128]{1,0:T(8,128)} %get-tuple-element.24.sv_t), custom_call_target="tpu_custom_call" | custom-call | tf_op jit(solution)/shard_map/finish/pallas_call | solution.py:497

commit v4 on v0

v4 whole, which is shorter than its diff:
```python
import functools
import math

import jax
import jax.numpy as jnp
from jax import lax
from jax.experimental import pallas as pl
from jax.experimental.pallas import tpu as pltpu
from jax.sharding import PartitionSpec as P

MESH = pl.DeviceIdType.MESH
F32 = jnp.float32
BF16 = jnp.bfloat16
HI = 16
LO = 16
NDEV = HI * LO
COLS = 4
REACH = 8
SINK_SLOT = REACH + 1
TOK = 256
DH = 128
HEADS = 16
SCALE = DH ** (-0.5)
EXP2_SCALE = SCALE * math.log2(math.e)


def place(device):
    device = (device + NDEV) % NDEV
    return (device // LO, device % LO)


def whoami():
    hi, lo = lax.axis_index("seqhi"), lax.axis_index("seqlo")
    return hi, lo, hi * LO + lo


def greet(targets):
    barrier = pltpu.get_barrier_semaphore()
    for target in targets:
        pl.semaphore_signal(barrier, inc=1, device_id=target, device_id_type=MESH)
    pl.semaphore_wait(barrier, len(targets))


def nt_dot(a, b):
    return lax.dot_general(a, b, (((1,), (1,)), ((), ())), preferred_element_type=F32)


def dot(a, b):
    return jnp.dot(a, b, preferred_element_type=F32)


def split3(x):
    first = x.astype(BF16)
    rest = x - first.astype(F32)
    second = rest.astype(BF16)
    third = (rest - second.astype(F32)).astype(BF16)
    return first, second, third


def back_of(step, col):
    group, at = (step - 1) // COLS * COLS, (step - 1) % COLS
    back = group + jnp.where(at < col, at + 1, jnp.where(at == col, COLS, at))
    return jnp.where(step > REACH, 0, back)


def fused_kernel(
    window, live, q_hbm, o_hbm, g_hbm, lse_ref, keys, values, sk_ref, sv_ref,
    dq_out, dk, dv, sk_out, sv_out,
    kv, acc, part, dq_acc, q_in, o_in, g_in, q_aug, g_aug, q_t, g_t, gaps, lse_cols, ds_a, p_a, ds_b, p_b,
    from_mates, from_near, from_far, sum_near, sum_far, sink_parts, sink_in, sink_mid, sink_sum, sink_buf, sink_all,
    load_sem, in_send, in_recv, out_send, out_recv, s_send, s_recv,
):
    hi, lo, me = whoami()
    col = me % COLS
    mates = [me - col + (col + j) % COLS for j in range(1, COLS)]
    cols = [(col + j) % COLS for j in range(1, COLS)]
    piece = DH * 2 // LO
    pairs = HEADS // 2

    loads = [
        pltpu.make_async_copy(keys, kv.at[REACH, 0], load_sem.at[0]),
        pltpu.make_async_copy(values, kv.at[REACH, 1], load_sem.at[1]),
        pltpu.make_async_copy(q_hbm, q_in, load_sem.at[2]),
        pltpu.make_async_copy(g_hbm, g_in, load_sem.at[3]),
        pltpu.make_async_copy(o_hbm, o_in, load_sem.at[4]),
    ]
    for copy in loads:
        copy.start()

    barrier = pltpu.get_barrier_semaphore()
    for target in [place(me + d) for d in (COLS, -COLS, REACH, -REACH)]:
        pl.semaphore_signal(barrier, inc=1, device_id=target, device_id_type=MESH)

    def greet_group(i, carry):
        pl.semaphore_signal(barrier, inc=1, device_id=(hi, (lo + i) % LO), device_id_type=MESH)
        pl.semaphore_signal(barrier, inc=1, device_id=((hi + i) % HI, lo), device_id_type=MESH)
        return carry

    lax.fori_loop(1, LO, greet_group, 0)
    pl.semaphore_wait(barrier, 4 + 15 + 15)

    def send_in(source, slot, target, index):
        return pltpu.make_async_remote_copy(
            src_ref=kv.at[source], dst_ref=kv.at[slot],
            send_sem=in_send.at[index], recv_sem=in_recv.at[slot],
            device_id=place(target), device_id_type=MESH,
        )

    loads[0].wait()
    loads[1].wait()
    send_in(REACH, 4, me + COLS, 0).start()
    for j in range(3):
        @pl.when(cols[j] > col)
        def _():
            send_in(REACH, REACH - (cols[j] - col), mates[j], 1 + j).start()

    def pass_near():
        send_in(4, 4, me + COLS, 0).wait_recv()
        send_in(4, 0, me + COLS, 4).start()
        for j in range(3):
            send_in(4, 4 - (cols[j] - col), mates[j], 5 + j).start()

    def pass_far():
        send_in(0, 0, me + COLS, 4).wait_recv()
        for j in range(3):
            @pl.when(cols[j] < col)
            def _():
                send_in(0, col - cols[j], mates[j], 1 + j).start()

    def send_out(back, target):
        near = jnp.where((back > col) & (back <= col + COLS), 0, 1)
        at = back % COLS - 1
        return pltpu.make_async_remote_copy(
            src_ref=part.at[REACH - back], dst_ref=from_mates.at[near, at],
            send_sem=out_send.at[back], recv_sem=out_recv.at[near, at],
            device_id=place(target), device_id_type=MESH,
        )

    def mate_arrival(kind, j):
        return pltpu.make_async_remote_copy(
            src_ref=part.at[0], dst_ref=from_mates.at[kind, j],
            send_sem=out_send.at[1], recv_sem=out_recv.at[kind, j],
            device_id=place(mates[j]), device_id_type=MESH,
        )

    def send_sum(source, dest, target, index):
        return pltpu.make_async_remote_copy(
            src_ref=source, dst_ref=dest, send_sem=out_send.at[index], recv_sem=out_recv.at[index // 4 - 1, 3],
            device_id=place(target), device_id_type=MESH,
        )

    near_send = send_sum(sum_near, from_near, me - COLS, 4)
    far_send = send_sum(sum_far, from_far, me - REACH, 8)

    def flush(step):
        back = back_of(step, col)
        slot = REACH - back

        @pl.when(step <= REACH)
        def _():
            part[slot, 0] = (acc[slot, 0] * SCALE).astype(BF16)
            part[slot, 1] = acc[slot, 1].astype(BF16)

        @pl.when((back != 0) & (back != 4) & (back != 8))
        def _():
            send_out(back, me - col + (col - back + 2 * COLS) % COLS).start()

    def exchange(phase, source, dest, along_lo):
        def copy(i, arriving):
            base = lo if along_lo else hi
            index = (base + i) % LO
            target = (hi, index) if along_lo else (index, lo)
            mine = index if arriving else base
            return pltpu.make_async_remote_copy(
                src_ref=source(index), dst_ref=dest(mine),
                send_sem=s_send.at[phase, i], recv_sem=s_recv.at[phase, mine],
                device_id=target, device_id_type=MESH,
            )

        def start():
            def body(i, carry):
                copy(i, False).start()
                return carry
            lax.fori_loop(1, LO, body, 0)

        def finish():
            def body(i, carry):
                copy(i, True).wait_recv()
                copy(i, False).wait_send()
                return carry
            lax.fori_loop(1, LO, body, 0)

        return start, finish

    start1, finish1 = exchange(0, lambda i: sink_parts.at[i], lambda i: sink_in.at[i], True)
    start2, finish2 = exchange(1, lambda i: sink_sum, lambda i: sink_mid.at[i], False)
    start3, finish3 = exchange(2, lambda i: sink_buf, lambda i: sink_all.at[i], True)

    def sum_of(ref):
        def body(i, total):
            return total + ref[i]
        return lax.fori_loop(1, LO, body, ref[0])

    def sink_begin():
        half = LO // 2
        sink_parts[:half] = (acc[SINK_SLOT, 0, :, :DH] * SCALE).reshape(half, piece, DH)
        sink_parts[half:] = acc[SINK_SLOT, 1, :, :DH].reshape(half, piece, DH)
        start1()

    def sink_second():
        finish1()
        sink_in[lo] = sink_parts[lo]
        sink_sum[...] = sum_of(sink_in)
        start2()

    def sink_third():
        finish2()
        sink_mid[hi] = sink_sum[...]
        sink_buf[...] = sum_of(sink_mid)
        start3()

    acc[...] = jnp.zeros_like(acc)
    dq_acc[...] = jnp.zeros_like(dq_acc)
    kv[SINK_SLOT] = jnp.zeros((2, TOK, DH), BF16)
    kv[SINK_SLOT, 0, :DH] = sk_ref[...]
    kv[SINK_SLOT, 1, :DH] = sv_ref[...]
    row_at = lax.broadcasted_iota(jnp.int32, (TOK, TOK), 0)
    col_at = lax.broadcasted_iota(jnp.int32, (TOK, TOK), 1)
    gaps[0] = row_at - col_at
    gaps[1] = col_at - row_at
    gaps[2] = col_at

    pieces = jnp.concatenate(split3(lse_ref[...] * (-1.0 / SCALE)), axis=0)
    row = lax.broadcasted_iota(jnp.int32, (3 * HEADS, DH), 0)
    column = lax.broadcasted_iota(jnp.int32, (3 * HEADS, DH), 1)
    pick = (row == column).astype(BF16)
    lse_cols[...] = lax.dot_general(
        pieces, pick, (((0,), (0,)), ((), ())), preferred_element_type=F32
    )
    for copy in loads[2:]:
        copy.wait()
    lane = lax.broadcasted_iota(jnp.int32, (TOK, DH), 1)

    def prepare(head, carry):
        at = pl.ds(pl.multiple_of(head * DH, DH), DH)
        q = q_in[:, at]
        g = g_in[:, at]
        delta = jnp.sum(g.astype(F32) * o_in[:, at].astype(F32), axis=1, keepdims=True)
        d1, d2, d3 = split3(-delta)
        minus_delta = jnp.where(
            lane == 0, d1.astype(F32),
            jnp.where(lane == 1, d2.astype(F32), jnp.where(lane == 2, d3.astype(F32), 0.0)),
        ).astype(BF16)
        minus_lse = jnp.where(lane % HEADS == head, lse_cols[...], 0.0).astype(BF16)
        q_aug[head, :, :DH] = q
        q_aug[head, :, DH:] = minus_lse
        g_aug[head, :, :DH] = g
        g_aug[head, :, DH:] = minus_delta
        q_t[head] = q.T
        g_t[head] = g.T
        return carry

    lax.fori_loop(0, HEADS, prepare, 0)
    ones = jnp.ones((TOK, DH), BF16)

    def slot_of(step):
        return jnp.where(step == 0, SINK_SLOT, REACH - back_of(step, col))

    def scores(step, pair, ds_buf, p_buf):
        back = back_of(step, col)
        sink = step == 0
        slot = slot_of(step)
        kind = jnp.where(sink, 2, jnp.where(back == 0, 1, 0))

        def limit(head):
            inside = jnp.where(back == 0, 1, window[head] - back * TOK)
            return jnp.where(sink, live[head], jnp.where(back <= me, inside, -(1 << 20)))

        q = q_aug[pl.ds(2 * pair, 2)].reshape(2 * TOK, 2 * DH)
        g = g_aug[pl.ds(2 * pair, 2)].reshape(2 * TOK, 2 * DH)
        s = nt_dot(q, jnp.concatenate([kv[slot, 0], ones], axis=1))
        dp = nt_dot(g, jnp.concatenate([kv[slot, 1], ones], axis=1))
        p = jnp.exp2(s * EXP2_SCALE)
        gap = gaps[kind]
        inside = jnp.concatenate([gap < limit(2 * pair), gap < limit(2 * pair + 1)], axis=0)
        p = jnp.where(inside, p, 0.0)
        ds_buf[...] = (p * dp).astype(BF16)
        p_buf[...] = p.astype(BF16)

    def gradients(step, pair, ds_buf, p_buf):
        slot = slot_of(step)
        ds = ds_buf[...]
        p = p_buf[...]
        dq = dot(ds, kv[slot, 0])
        dk_t = dot(jnp.concatenate([q_t[2 * pair], q_t[2 * pair + 1]], axis=1), ds)
        dv_t = dot(jnp.concatenate([g_t[2 * pair], g_t[2 * pair + 1]], axis=1), p)
        dq_acc[2 * pair] += dq[:TOK]
        dq_acc[2 * pair + 1] += dq[TOK:]
        acc[slot, 0] += dk_t
        acc[slot, 1] += dv_t

    half_pairs = pairs // 2
    scores(0, 0, ds_a, p_a)

    def body(it, carry):
        step, at = it // half_pairs, it % half_pairs

        @pl.when(at == 0)
        def _():
            @pl.when(step == 1)
            def _():
                sink_begin()

            @pl.when(step == 3)
            def _():
                sink_second()

            @pl.when(step == 5)
            def _():
                sink_third()

            @pl.when(step >= 2)
            def _():
                flush(step - 1)

        @pl.when(at == half_pairs - 1)
        def _():
            @pl.when(step == 0)
            def _():
                pass_near()

            @pl.when(step == 3)
            def _():
                pass_far()

            back = back_of(step + 1, col)

            @pl.when((step + 1 <= REACH) & (back != 4) & (back != 8))
            def _():
                send_in(4, REACH - back, me, 0).wait_recv()

        last = at == half_pairs - 1
        next_step = jnp.minimum(jnp.where(last, step + 1, step), REACH + 1)
        next_pair = jnp.where(last, 0, 2 * at + 2)
        scores(step, 2 * at + 1, ds_b, p_b)
        gradients(step, 2 * at, ds_a, p_a)
        scores(next_step, next_pair, ds_a, p_a)
        gradients(step, 2 * at + 1, ds_b, p_b)
        return carry

    lax.fori_loop(0, (REACH + 2) * half_pairs, body, 0)

    for j in range(3):
        mate_arrival(0, j).wait_recv()
        mate_arrival(1, j).wait_recv()
    for half in range(2):
        total = part[0, half].astype(F32)
        for j in range(3):
            total = total + jnp.where(cols[j] < col, from_mates[1, j, half].astype(F32), 0.0)
        sum_far[half] = total.astype(BF16)
    far_send.start()
    for half in range(2):
        total = part[REACH - 4, half].astype(F32)
        for j in range(3):
            total = total + from_mates[0, j, half].astype(F32)
        sum_near[half] = total.astype(BF16)
    near_send.start()

    for head in range(HEADS):
        dq_out[:, head * DH:(head + 1) * DH] = dq_acc[head] * SCALE

    finish3()
    sink_all[lo] = sink_buf[...]
    for i in range(LO // 2):
        sk_out[i * piece:(i + 1) * piece, :] = sink_all[i]
        sv_out[i * piece:(i + 1) * piece, :] = sink_all[LO // 2 + i]

    near_send.wait_recv()
    far_send.wait_recv()
    for half in range(2):
        total = acc[REACH, half]
        if half == 0:
            total = total * SCALE
        total = total + from_near[half].astype(F32) + from_far[half].astype(F32)
        for j in range(3):
            total = total + jnp.where(cols[j] > col, from_mates[1, j, half].astype(F32), 0.0)
        if half == 0:
            dk[...] = total.T
        else:
            dv[...] = total.T

    for index in range(8):
        send_in(REACH, 4, me + COLS, index).wait_send()
    for back in (1, 2, 3, 5, 6, 7):
        pltpu.make_async_remote_copy(
            src_ref=part.at[REACH - back], dst_ref=from_mates.at[0, 0],
            send_sem=out_send.at[back], recv_sem=out_recv.at[0, 0],
            device_id=place(me + COLS), device_id_type=MESH,
        ).wait_send()
    near_send.wait_send()
    far_send.wait_send()


def fused(queries, outputs, out_grad, lse, keys, values, sink_keys, sink_values, window_len, sink_live):
    smem = pl.BlockSpec(memory_space=pltpu.SMEM)
    vmem = pl.BlockSpec(memory_space=pltpu.VMEM)
    hbm = pl.BlockSpec(memory_space=pl.ANY)
    piece = DH * 2 // LO
    block = (2, DH, TOK)
    wide = (HEADS, TOK, 2 * DH)
    return pl.pallas_call(
        fused_kernel,
        out_shape=(
            jax.ShapeDtypeStruct((TOK, HEADS * DH), F32),
            jax.ShapeDtypeStruct((TOK, DH), F32),
            jax.ShapeDtypeStruct((TOK, DH), F32),
            jax.ShapeDtypeStruct((DH, DH), F32),
            jax.ShapeDtypeStruct((DH, DH), F32),
        ),
        in_specs=[smem] * 2 + [hbm] * 3 + [vmem] + [hbm] * 2 + [vmem] * 2,
        out_specs=(vmem,) * 5,
        scratch_shapes=[
            pltpu.VMEM((SINK_SLOT + 1, 2, TOK, DH), BF16),
            pltpu.VMEM((SINK_SLOT + 1,) + block, F32),
            pltpu.VMEM((REACH,) + block, BF16),
            pltpu.VMEM((HEADS, TOK, DH), F32),
            pltpu.VMEM((TOK, HEADS * DH), BF16),
            pltpu.VMEM((TOK, HEADS * DH), BF16),
            pltpu.VMEM((TOK, HEADS * DH), BF16),
            pltpu.VMEM(wide, BF16),
            pltpu.VMEM(wide, BF16),
            pltpu.VMEM((HEADS, DH, TOK), BF16),
            pltpu.VMEM((HEADS, DH, TOK), BF16),
            pltpu.VMEM((3, TOK, TOK), jnp.int32),
            pltpu.VMEM((TOK, DH), F32),
        ]
        + [pltpu.VMEM((2 * TOK, TOK), BF16)] * 4
        + [pltpu.VMEM((2, 3) + block, BF16)]
        + [pltpu.VMEM(block, BF16)] * 4
        + [
            pltpu.VMEM((LO, piece, DH), F32),
            pltpu.VMEM((LO, piece, DH), F32),
            pltpu.VMEM((HI, piece, DH), F32),
            pltpu.VMEM((piece, DH), F32),
            pltpu.VMEM((piece, DH), F32),
            pltpu.VMEM((LO, piece, DH), F32),
            pltpu.SemaphoreType.DMA((5,)),
            pltpu.SemaphoreType.DMA((8,)),
            pltpu.SemaphoreType.DMA((REACH + 1,)),
            pltpu.SemaphoreType.DMA((REACH + 1,)),
            pltpu.SemaphoreType.DMA((2, 4)),
            pltpu.SemaphoreType.DMA((3, LO)),
            pltpu.SemaphoreType.DMA((3, LO)),
        ],
        compiler_params=pltpu.CompilerParams(collective_id=0, has_side_effects=True),
        name="window_backward",
    )(window_len, sink_live, queries, outputs, out_grad, lse, keys, values, sink_keys, sink_values)


def finish_kernel(dk, dv, sk_t, sv_t, dk_out, dv_out, sk_out, sv_out):
    dk_out[...] = dk[...]
    dv_out[...] = dv[...]
    sk_out[...] = sk_t[...].T
    sv_out[...] = sv_t[...].T


def finish(dk, dv, sk_t, sv_t):
    vmem = pl.BlockSpec(memory_space=pltpu.VMEM)
    return pl.pallas_call(
        finish_kernel,
        out_shape=[jax.ShapeDtypeStruct(x.shape, F32) for x in (dk, dv, sk_t, sv_t)],
        in_specs=[vmem] * 4,
        out_specs=[vmem] * 4,
        name="finish",
    )(dk, dv, sk_t, sv_t)


def on_device(
    queries, keys, values, outputs, out_grad, lse, sink_keys, sink_values, window_len, sink_live
):
    query_grad, key_grad, value_grad, sk_t, sv_t = fused(
        queries, outputs, out_grad, lse, keys, values, sink_keys, sink_values, window_len, sink_live
    )
    return (query_grad,) + tuple(finish(key_grad, value_grad, sk_t, sv_t))


def solution(mesh):
    rows = P(("seqhi", "seqlo"), None)
    return jax.shard_map(
        on_device,
        mesh=mesh,
        in_specs=(rows, rows, rows, rows, rows, P(None, ("seqhi", "seqlo")), P(), P(), P(), P()),
        out_specs=(rows, rows, rows, P(), P()),
        check_vma=False,
    )
```

time: 474 us -> 76.4 us (0.16)
  the two profiles are of different devices: /device:TPU:32 before, /device:TPU:73 now
where the time goes in v4:
time: 76.4 us; the launch traced here: 76.2 us
  Pallas kernels  72.4 us (95%)
  local copies, waits for them, and re-layouts  3.14 us (4%)
    pallas_call x1, Pallas kernels, fused(): pl.pallas_call(fused_kernel, out_shape=(jax.ShapeDtypeStruct((TOK, HEADS...  70.6 us
    unnamed x1, local copies, waits for them, and re-layouts  3.14 us
    pallas_call x1, Pallas kernels, finish(): pl.pallas_call(finish_kernel, out_shape=[jax.ShapeDtypeStruct(x.shape, F3...  1.75 us

profile of v4, /device:TPU:73, one launch (start us, length us, event | category | flops | bytes accessed | tf_op | source)
XLA Modules:
  0.0 76.2 jit_solution(17339009918404368688)
XLA Ops:
  0.6 70.6 %window_backward.1 = (f32[256,2048]{1,0:T(8,128)}, f32[256,128]{1,0:T(8,128)}, f32[256,128]{1,0:T(8,128)}, f32[128,128]{1,0:T(8,128)}, f32[128,128]{1,0:T(8,128)}) custom-call(s32[16]{0:T(128)} %window.1, s32[16]{0:T(128)} %live.1, bf16[256,2048]{1,0:T(8,128)(2,1)} %q_hbm.1, bf16[256,2048]{1,0:T(8,128)(2,1)} %o_hbm.1, bf16[256,2048]{1,0:T(8,128)(2,1)} %g_hbm.1, ...), custom_call_target="tpu_custom_call" | custom-call | tf_op jit(solution)/shard_map/window_backward/pallas_call | solution.py:411
  71.3 1.8 %finish.1 = (f32[256,128]{1,0:T(8,128)}, f32[256,128]{1,0:T(8,128)}, f32[128,128]{1,0:T(8,128)}, f32[128,128]{1,0:T(8,128)}) custom-call(f32[256,128]{1,0:T(8,128)} %get-tuple-element.15.dk, f32[256,128]{1,0:T(8,128)} %get-tuple-element.16.dv, f32[128,128]{1,0:T(8,128)} %get-tuple-element.17.sk_t, f32[128,128]{1,0:T(8,128)} %get-tuple-element.18.sv_t), custom_call_target="tpu_custom_call" | custom-call | tf_op jit(solution)/shard_map/finish/pallas_call | solution.py:469
  73.0 3.1 %copy.16 = f32[256,2048]{1,0:T(8,128)} copy(f32[256,2048]{1,0:T(8,128)} %get-tuple-element.28) | data formatting | bytes 4194304

commit v5 on v4

--- a/solution.py
+++ b/solution.py
@@ -17,6 +17,8 @@
 COLS = 4
 REACH = 8
 SINK_SLOT = REACH + 1
+UNROLL = 4
+FAR_STEP = 2
 TOK = 256
 DH = 128
 HEADS = 16
@@ -66,7 +68,7 @@
 def fused_kernel(
     window, live, q_hbm, o_hbm, g_hbm, lse_ref, keys, values, sk_ref, sv_ref,
     dq_out, dk, dv, sk_out, sv_out,
-    kv, acc, part, dq_acc, q_in, o_in, g_in, q_aug, g_aug, q_t, g_t, gaps, lse_cols, ds_a, p_a, ds_b, p_b,
+    kv, acc, part, dq_acc, dq_stage, q_in, o_in, g_in, q_heads, g_heads, q_t, g_t, gaps, lse_rep, delta_rep, ds_a, p_a, ds_b, p_b,
     from_mates, from_near, from_far, sum_near, sum_far, sink_parts, sink_in, sink_mid, sink_sum, sink_buf, sink_all,
     load_sem, in_send, in_recv, out_send, out_recv, s_send, s_recv,
 ):
@@ -97,6 +99,17 @@
         return carry
 
     lax.fori_loop(1, LO, greet_group, 0)
+    acc[...] = jnp.zeros_like(acc)
+    dq_acc[...] = jnp.zeros_like(dq_acc)
+    kv[SINK_SLOT] = jnp.zeros((2, TOK, DH), BF16)
+    kv[SINK_SLOT, 0, :DH] = sk_ref[...]
+    kv[SINK_SLOT, 1, :DH] = sv_ref[...]
+    row_at = lax.broadcasted_iota(jnp.int32, (TOK, TOK), 0)
+    col_at = lax.broadcasted_iota(jnp.int32, (TOK, TOK), 1)
+    gaps[0] = row_at - col_at
+    gaps[1] = col_at - row_at
+    gaps[2] = col_at
+
     pl.semaphore_wait(barrier, 4 + 15 + 15)
 
     def send_in(source, slot, target, index):
@@ -219,76 +232,51 @@
         sink_buf[...] = sum_of(sink_mid)
         start3()
 
-    acc[...] = jnp.zeros_like(acc)
-    dq_acc[...] = jnp.zeros_like(dq_acc)
-    kv[SINK_SLOT] = jnp.zeros((2, TOK, DH), BF16)
-    kv[SINK_SLOT, 0, :DH] = sk_ref[...]
-    kv[SINK_SLOT, 1, :DH] = sv_ref[...]
-    row_at = lax.broadcasted_iota(jnp.int32, (TOK, TOK), 0)
-    col_at = lax.broadcasted_iota(jnp.int32, (TOK, TOK), 1)
-    gaps[0] = row_at - col_at
-    gaps[1] = col_at - row_at
-    gaps[2] = col_at
-
-    pieces = jnp.concatenate(split3(lse_ref[...] * (-1.0 / SCALE)), axis=0)
+    pieces = jnp.concatenate(split3(lse_ref[...] * math.log2(math.e)), axis=0)
     row = lax.broadcasted_iota(jnp.int32, (3 * HEADS, DH), 0)
-    column = lax.broadcasted_iota(jnp.int32, (3 * HEADS, DH), 1)
-    pick = (row == column).astype(BF16)
-    lse_cols[...] = lax.dot_general(
-        pieces, pick, (((0,), (0,)), ((), ())), preferred_element_type=F32
-    )
     for copy in loads[2:]:
         copy.wait()
-    lane = lax.broadcasted_iota(jnp.int32, (TOK, DH), 1)
-
     def prepare(head, carry):
         at = pl.ds(pl.multiple_of(head * DH, DH), DH)
         q = q_in[:, at]
         g = g_in[:, at]
         delta = jnp.sum(g.astype(F32) * o_in[:, at].astype(F32), axis=1, keepdims=True)
-        d1, d2, d3 = split3(-delta)
-        minus_delta = jnp.where(
-            lane == 0, d1.astype(F32),
-            jnp.where(lane == 1, d2.astype(F32), jnp.where(lane == 2, d3.astype(F32), 0.0)),
-        ).astype(BF16)
-        minus_lse = jnp.where(lane % HEADS == head, lse_cols[...], 0.0).astype(BF16)
-        q_aug[head, :, :DH] = q
-        q_aug[head, :, DH:] = minus_lse
-        g_aug[head, :, :DH] = g
-        g_aug[head, :, DH:] = minus_delta
+        delta_rep[head] = jnp.broadcast_to(delta, (TOK, DH))
+        pick = (row % HEADS == head).astype(BF16)
+        lse_rep[head] = lax.dot_general(
+            pieces, pick, (((0,), (0,)), ((), ())), preferred_element_type=F32
+        )
+        q_heads[head] = q
+        g_heads[head] = g
         q_t[head] = q.T
         g_t[head] = g.T
         return carry
 
     lax.fori_loop(0, HEADS, prepare, 0)
-    ones = jnp.ones((TOK, DH), BF16)
 
     def slot_of(step):
         return jnp.where(step == 0, SINK_SLOT, REACH - back_of(step, col))
 
-    def scores(step, pair, ds_buf, p_buf):
-        back = back_of(step, col)
-        sink = step == 0
-        slot = slot_of(step)
-        kind = jnp.where(sink, 2, jnp.where(back == 0, 1, 0))
-
-        def limit(head):
+    def twice(x):
+        return jnp.concatenate([x, x], axis=1)
+
+    def scores(slot, pair, ds_buf, p_buf):
+        back = REACH - slot
+        kind = jnp.where(back < 0, 2, jnp.where(back == 0, 1, 0))
+        gap = gaps[kind]
+        s = nt_dot(q_heads[pl.ds(2 * pair, 2)].reshape(2 * TOK, DH), kv[slot, 0])
+        dp = nt_dot(g_heads[pl.ds(2 * pair, 2)].reshape(2 * TOK, DH), kv[slot, 1])
+        for u in range(2):
+            head = 2 * pair + u
             inside = jnp.where(back == 0, 1, window[head] - back * TOK)
-            return jnp.where(sink, live[head], jnp.where(back <= me, inside, -(1 << 20)))
-
-        q = q_aug[pl.ds(2 * pair, 2)].reshape(2 * TOK, 2 * DH)
-        g = g_aug[pl.ds(2 * pair, 2)].reshape(2 * TOK, 2 * DH)
-        s = nt_dot(q, jnp.concatenate([kv[slot, 0], ones], axis=1))
-        dp = nt_dot(g, jnp.concatenate([kv[slot, 1], ones], axis=1))
-        p = jnp.exp2(s * EXP2_SCALE)
-        gap = gaps[kind]
-        inside = jnp.concatenate([gap < limit(2 * pair), gap < limit(2 * pair + 1)], axis=0)
-        p = jnp.where(inside, p, 0.0)
-        ds_buf[...] = (p * dp).astype(BF16)
-        p_buf[...] = p.astype(BF16)
-
-    def gradients(step, pair, ds_buf, p_buf):
-        slot = slot_of(step)
+            limit = jnp.where(back < 0, live[head], jnp.where(back <= me, inside, -(1 << 20)))
+            at = slice(u * TOK, (u + 1) * TOK)
+            p = jnp.exp2(s[at] * EXP2_SCALE - twice(lse_rep[head]))
+            p = jnp.where(gap < limit, p, 0.0)
+            ds_buf[at] = (p * (dp[at] - twice(delta_rep[head]))).astype(BF16)
+            p_buf[at] = p.astype(BF16)
+
+    def gradients(slot, pair, ds_buf, p_buf):
         ds = ds_buf[...]
         p = p_buf[...]
         dq = dot(ds, kv[slot, 0])
@@ -299,11 +287,22 @@
         acc[slot, 0] += dk_t
         acc[slot, 1] += dv_t
 
-    half_pairs = pairs // 2
-    scores(0, 0, ds_a, p_a)
+    turns = pairs // UNROLL
+    scores(SINK_SLOT, 0, ds_a, p_a)
+
+    def sum_near_and_send():
+        for j in range(3):
+            mate_arrival(0, j).wait_recv()
+        for half in range(2):
+            total = part[REACH - 4, half].astype(F32)
+            for j in range(3):
+                total = total + from_mates[0, j, half].astype(F32)
+            sum_near[half] = total.astype(BF16)
+        near_send.start()
 
     def body(it, carry):
-        step, at = it // half_pairs, it % half_pairs
+        slot, next_slot = carry
+        step, at = it // turns, it % turns
 
         @pl.when(at == 0)
         def _():
@@ -323,35 +322,40 @@
             def _():
                 flush(step - 1)
 
-        @pl.when(at == half_pairs - 1)
+        @pl.when(at == turns - 1)
         def _():
             @pl.when(step == 0)
             def _():
                 pass_near()
 
-            @pl.when(step == 3)
+            @pl.when(step == FAR_STEP)
             def _():
                 pass_far()
 
+            @pl.when(step == REACH + 1)
+            def _():
+                sum_near_and_send()
+
             back = back_of(step + 1, col)
 
             @pl.when((step + 1 <= REACH) & (back != 4) & (back != 8))
             def _():
                 send_in(4, REACH - back, me, 0).wait_recv()
 
-        last = at == half_pairs - 1
-        next_step = jnp.minimum(jnp.where(last, step + 1, step), REACH + 1)
-        next_pair = jnp.where(last, 0, 2 * at + 2)
-        scores(step, 2 * at + 1, ds_b, p_b)
-        gradients(step, 2 * at, ds_a, p_a)
-        scores(next_step, next_pair, ds_a, p_a)
-        gradients(step, 2 * at + 1, ds_b, p_b)
-        return carry
-
-    lax.fori_loop(0, (REACH + 2) * half_pairs, body, 0)
+        last = at == turns - 1
+        first = UNROLL * at
+        buffers = ((ds_a, p_a), (ds_b, p_b))
+        for u in range(UNROLL):
+            if u < UNROLL - 1:
+                scores(slot, first + u + 1, *buffers[(u + 1) % 2])
+            else:
+                scores(jnp.where(last, next_slot, slot), jnp.where(last, 0, first + UNROLL), *buffers[0])
+            gradients(slot, first + u, *buffers[u % 2])
+        return jnp.where(last, next_slot, slot), jnp.where(last, slot_of(jnp.minimum(step + 2, REACH + 1)), next_slot)
+
+    lax.fori_loop(0, (REACH + 2) * turns, body, (jnp.int32(SINK_SLOT), slot_of(1)))
 
     for j in range(3):
-        mate_arrival(0, j).wait_recv()
         mate_arrival(1, j).wait_recv()
     for half in range(2):
         total = part[0, half].astype(F32)
@@ -359,21 +363,15 @@
             total = total + jnp.where(cols[j] < col, from_mates[1, j, half].astype(F32), 0.0)
         sum_far[half] = total.astype(BF16)
     far_send.start()
-    for half in range(2):
-        total = part[REACH - 4, half].astype(F32)
-        for j in range(3):
-            total = total + from_mates[0, j, half].astype(F32)
-        sum_near[half] = total.astype(BF16)
-    near_send.start()
-
     for head in range(HEADS):
-        dq_out[:, head * DH:(head + 1) * DH] = dq_acc[head] * SCALE
+        dq_stage[:, head * DH:(head + 1) * DH] = dq_acc[head] * SCALE
+    dq_copy = pltpu.make_async_copy(dq_stage, dq_out, load_sem.at[0])
+    dq_copy.start()
 
     finish3()
     sink_all[lo] = sink_buf[...]
-    for i in range(LO // 2):
-        sk_out[i * piece:(i + 1) * piece, :] = sink_all[i]
-        sv_out[i * piece:(i + 1) * piece, :] = sink_all[LO // 2 + i]
+    sk_out[...] = sink_all[:LO // 2].reshape(DH, DH).T
+    sv_out[...] = sink_all[LO // 2:].reshape(DH, DH).T
 
     near_send.wait_recv()
     far_send.wait_recv()
@@ -399,15 +397,17 @@
         ).wait_send()
     near_send.wait_send()
     far_send.wait_send()
+    dq_copy.wait()
 
 
 def fused(queries, outputs, out_grad, lse, keys, values, sink_keys, sink_values, window_len, sink_live):
     smem = pl.BlockSpec(memory_space=pltpu.SMEM)
     vmem = pl.BlockSpec(memory_space=pltpu.VMEM)
-    hbm = pl.BlockSpec(memory_space=pl.ANY)
+    hbm = pl.BlockSpec(memory_space=pltpu.HBM)
+    anywhere = pl.BlockSpec(memory_space=pl.ANY)
     piece = DH * 2 // LO
     block = (2, DH, TOK)
-    wide = (HEADS, TOK, 2 * DH)
+    wide = (HEADS, TOK, DH)
     return pl.pallas_call(
         fused_kernel,
         out_shape=(
@@ -418,12 +418,13 @@
             jax.ShapeDtypeStruct((DH, DH), F32),
         ),
         in_specs=[smem] * 2 + [hbm] * 3 + [vmem] + [hbm] * 2 + [vmem] * 2,
-        out_specs=(vmem,) * 5,
+        out_specs=(anywhere,) + (vmem,) * 4,
         scratch_shapes=[
             pltpu.VMEM((SINK_SLOT + 1, 2, TOK, DH), BF16),
             pltpu.VMEM((SINK_SLOT + 1,) + block, F32),
             pltpu.VMEM((REACH,) + block, BF16),
             pltpu.VMEM((HEADS, TOK, DH), F32),
+            pltpu.VMEM((TOK, HEADS * DH), F32),
             pltpu.VMEM((TOK, HEADS * DH), BF16),
             pltpu.VMEM((TOK, HEADS * DH), BF16),
             pltpu.VMEM((TOK, HEADS * DH), BF16),
@@ -432,7 +433,8 @@
             pltpu.VMEM((HEADS, DH, TOK), BF16),
             pltpu.VMEM((HEADS, DH, TOK), BF16),
             pltpu.VMEM((3, TOK, TOK), jnp.int32),
-            pltpu.VMEM((TOK, DH), F32),
+            pltpu.VMEM(wide, F32),
+            pltpu.VMEM(wide, F32),
         ]
         + [pltpu.VMEM((2 * TOK, TOK), BF16)] * 4
         + [pltpu.VMEM((2, 3) + block, BF16)]
@@ -452,36 +454,46 @@
             pltpu.SemaphoreType.DMA((3, LO)),
             pltpu.SemaphoreType.DMA((3, LO)),
         ],
-        compiler_params=pltpu.CompilerParams(collective_id=0, has_side_effects=True),
+        compiler_params=pltpu.CompilerParams(
+            collective_id=0, has_side_effects=True, vmem_limit_bytes=36 << 20
+        ),
         name="window_backward",
-    )(window_len, sink_live, queries, outputs, out_grad, lse, keys, values, sink_keys, sink_values)
-
-
-def finish_kernel(dk, dv, sk_t, sv_t, dk_out, dv_out, sk_out, sv_out):
-    dk_out[...] = dk[...]
-    dv_out[...] = dv[...]
-    sk_out[...] = sk_t[...].T
-    sv_out[...] = sv_t[...].T
-
-
-def finish(dk, dv, sk_t, sv_t):
-    vmem = pl.BlockSpec(memory_space=pltpu.VMEM)
+    )(*[
+        pltpu.with_memory_space_constraint(x, pltpu.HBM)
+        for x in (window_len, sink_live, queries, outputs, out_grad, lse, keys, values, sink_keys, sink_values)
+    ])
+
+
+def finish_kernel(*refs):
+    count = len(refs) // 2
+    copies = [
+        pltpu.make_async_copy(refs[i], refs[count + i], refs[-1].at[i]) for i in range(count)
+    ]
+    for copy in copies:
+        copy.start()
+    for copy in copies:
+        copy.wait()
+
+
+def finish(*results):
+    anywhere = pl.BlockSpec(memory_space=pl.ANY)
     return pl.pallas_call(
         finish_kernel,
-        out_shape=[jax.ShapeDtypeStruct(x.shape, F32) for x in (dk, dv, sk_t, sv_t)],
-        in_specs=[vmem] * 4,
-        out_specs=[vmem] * 4,
+        out_shape=[jax.ShapeDtypeStruct(x.shape, F32) for x in results],
+        in_specs=[anywhere] * 5,
+        out_specs=[anywhere] * 5,
+        scratch_shapes=[pltpu.SemaphoreType.DMA((5,))],
+        compiler_params=pltpu.CompilerParams(vmem_limit_bytes=8 << 20),
         name="finish",
-    )(dk, dv, sk_t, sv_t)
+    )(*results)
 
 
 def on_device(
     queries, keys, values, outputs, out_grad, lse, sink_keys, sink_values, window_len, sink_live
 ):
-    query_grad, key_grad, value_grad, sk_t, sv_t = fused(
+    return tuple(finish(*fused(
         queries, outputs, out_grad, lse, keys, values, sink_keys, sink_values, window_len, sink_live
-    )
-    return (query_grad,) + tuple(finish(key_grad, value_grad, sk_t, sv_t))
+    )))
 
 
 def solution(mesh):

time: 76.4 us -> 67.1 us (0.88)
  the two profiles are of different devices: /device:TPU:73 before, /device:TPU:32 now
where the time goes in v5:
time: 67.1 us; the launch traced here: 66.9 us
  Pallas kernels  66.3 us (99%)
    pallas_call x1, Pallas kernels, fused(): pl.pallas_call(fused_kernel, out_shape=(jax.ShapeDtypeStruct((TOK, HEADS...  64.8 us
    pallas_call x1, Pallas kernels, finish(): pl.pallas_call(finish_kernel, out_shape=[jax.ShapeDtypeStruct(x.shape, F3...  1.47 us

profile of v5, /device:TPU:32, one launch (start us, length us, event | category | flops | bytes accessed | tf_op | source)
XLA Modules:
  0.0 66.9 jit_solution(5285844957468904298)
XLA Ops:
  0.6 64.8 %window_backward.1 = (f32[256,2048]{1,0:T(8,128)S(1)}, f32[256,128]{1,0:T(8,128)S(1)}, f32[256,128]{1,0:T(8,128)S(1)}, f32[128,128]{1,0:T(8,128)S(1)}, f32[128,128]{1,0:T(8,128)S(1)}) custom-call(s32[16]{0:T(128)} %window.1, s32[16]{0:T(128)} %live.1, bf16[256,2048]{1,0:T(8,128)(2,1)} %q_hbm.1, bf16[256,2048]{1,0:T(8,128)(2,1)} %o_hbm.1, ...), custom_call_target="tpu_custom_call" | custom-call | tf_op jit(solution)/shard_map/window_backward/pallas_call | solution.py:411
  65.4 1.5 %finish.1 = (f32[256,2048]{1,0:T(8,128)}, f32[256,128]{1,0:T(8,128)}, f32[256,128]{1,0:T(8,128)}, f32[128,128]{1,0:T(8,128)}, f32[128,128]{1,0:T(8,128)}) custom-call(f32[256,2048]{1,0:T(8,128)S(1)} %get-tuple-element.10.refs_0_, f32[256,128]{1,0:T(8,128)S(1)} %get-tuple-element.11.refs_1_, f32[256,128]{1,0:T(8,128)S(1)} %get-tuple-element.12.refs_2_, ...), custom_call_target="tpu_custom_call" | custom-call | tf_op jit(solution)/shard_map/finish/pallas_call | solution.py:480

commit v6 on v5

--- a/solution.py
+++ b/solution.py
@@ -19,6 +19,7 @@
 SINK_SLOT = REACH + 1
 UNROLL = 4
 FAR_STEP = 2
+EARLY = 10
 TOK = 256
 DH = 128
 HEADS = 16
@@ -109,128 +110,6 @@
     gaps[0] = row_at - col_at
     gaps[1] = col_at - row_at
     gaps[2] = col_at
-
-    pl.semaphore_wait(barrier, 4 + 15 + 15)
-
-    def send_in(source, slot, target, index):
-        return pltpu.make_async_remote_copy(
-            src_ref=kv.at[source], dst_ref=kv.at[slot],
-            send_sem=in_send.at[index], recv_sem=in_recv.at[slot],
-            device_id=place(target), device_id_type=MESH,
-        )
-
-    loads[0].wait()
-    loads[1].wait()
-    send_in(REACH, 4, me + COLS, 0).start()
-    for j in range(3):
-        @pl.when(cols[j] > col)
-        def _():
-            send_in(REACH, REACH - (cols[j] - col), mates[j], 1 + j).start()
-
-    def pass_near():
-        send_in(4, 4, me + COLS, 0).wait_recv()
-        send_in(4, 0, me + COLS, 4).start()
-        for j in range(3):
-            send_in(4, 4 - (cols[j] - col), mates[j], 5 + j).start()
-
-    def pass_far():
-        send_in(0, 0, me + COLS, 4).wait_recv()
-        for j in range(3):
-            @pl.when(cols[j] < col)
-            def _():
-                send_in(0, col - cols[j], mates[j], 1 + j).start()
-
-    def send_out(back, target):
-        near = jnp.where((back > col) & (back <= col + COLS), 0, 1)
-        at = back % COLS - 1
-        return pltpu.make_async_remote_copy(
-            src_ref=part.at[REACH - back], dst_ref=from_mates.at[near, at],
-            send_sem=out_send.at[back], recv_sem=out_recv.at[near, at],
-            device_id=place(target), device_id_type=MESH,
-        )
-
-    def mate_arrival(kind, j):
-        return pltpu.make_async_remote_copy(
-            src_ref=part.at[0], dst_ref=from_mates.at[kind, j],
-            send_sem=out_send.at[1], recv_sem=out_recv.at[kind, j],
-            device_id=place(mates[j]), device_id_type=MESH,
-        )
-
-    def send_sum(source, dest, target, index):
-        return pltpu.make_async_remote_copy(
-            src_ref=source, dst_ref=dest, send_sem=out_send.at[index], recv_sem=out_recv.at[index // 4 - 1, 3],
-            device_id=place(target), device_id_type=MESH,
-        )
-
-    near_send = send_sum(sum_near, from_near, me - COLS, 4)
-    far_send = send_sum(sum_far, from_far, me - REACH, 8)
-
-    def flush(step):
-        back = back_of(step, col)
-        slot = REACH - back
-
-        @pl.when(step <= REACH)
-        def _():
-            part[slot, 0] = (acc[slot, 0] * SCALE).astype(BF16)
-            part[slot, 1] = acc[slot, 1].astype(BF16)
-
-        @pl.when((back != 0) & (back != 4) & (back != 8))
-        def _():
-            send_out(back, me - col + (col - back + 2 * COLS) % COLS).start()
-
-    def exchange(phase, source, dest, along_lo):
-        def copy(i, arriving):
-            base = lo if along_lo else hi
-            index = (base + i) % LO
-            target = (hi, index) if along_lo else (index, lo)
-            mine = index if arriving else base
-            return pltpu.make_async_remote_copy(
-                src_ref=source(index), dst_ref=dest(mine),
-                send_sem=s_send.at[phase, i], recv_sem=s_recv.at[phase, mine],
-                device_id=target, device_id_type=MESH,
-            )
-
-        def start():
-            def body(i, carry):
-                copy(i, False).start()
-                return carry
-            lax.fori_loop(1, LO, body, 0)
-
-        def finish():
-            def body(i, carry):
-                copy(i, True).wait_recv()
-                copy(i, False).wait_send()
-                return carry
-            lax.fori_loop(1, LO, body, 0)
-
-        return start, finish
-
-    start1, finish1 = exchange(0, lambda i: sink_parts.at[i], lambda i: sink_in.at[i], True)
-    start2, finish2 = exchange(1, lambda i: sink_sum, lambda i: sink_mid.at[i], False)
-    start3, finish3 = exchange(2, lambda i: sink_buf, lambda i: sink_all.at[i], True)
-
-    def sum_of(ref):
-        def body(i, total):
-            return total + ref[i]
-        return lax.fori_loop(1, LO, body, ref[0])
-
-    def sink_begin():
-        half = LO // 2
-        sink_parts[:half] = (acc[SINK_SLOT, 0, :, :DH] * SCALE).reshape(half, piece, DH)
-        sink_parts[half:] = acc[SINK_SLOT, 1, :, :DH].reshape(half, piece, DH)
-        start1()
-
-    def sink_second():
-        finish1()
-        sink_in[lo] = sink_parts[lo]
-        sink_sum[...] = sum_of(sink_in)
-        start2()
-
-    def sink_third():
-        finish2()
-        sink_mid[hi] = sink_sum[...]
-        sink_buf[...] = sum_of(sink_mid)
-        start3()
 
     pieces = jnp.concatenate(split3(lse_ref[...] * math.log2(math.e)), axis=0)
     row = lax.broadcasted_iota(jnp.int32, (3 * HEADS, DH), 0)
@@ -252,7 +131,130 @@
         g_t[head] = g.T
         return carry
 
-    lax.fori_loop(0, HEADS, prepare, 0)
+    lax.fori_loop(0, EARLY, prepare, 0)
+    pl.semaphore_wait(barrier, 4 + 15 + 15)
+
+    def send_in(source, slot, target, index):
+        return pltpu.make_async_remote_copy(
+            src_ref=kv.at[source], dst_ref=kv.at[slot],
+            send_sem=in_send.at[index], recv_sem=in_recv.at[slot],
+            device_id=place(target), device_id_type=MESH,
+        )
+
+    loads[0].wait()
+    loads[1].wait()
+    send_in(REACH, 4, me + COLS, 0).start()
+    for j in range(3):
+        @pl.when(cols[j] > col)
+        def _():
+            send_in(REACH, REACH - (cols[j] - col), mates[j], 1 + j).start()
+
+    def pass_near():
+        send_in(4, 4, me + COLS, 0).wait_recv()
+        send_in(4, 0, me + COLS, 4).start()
+        for j in range(3):
+            send_in(4, 4 - (cols[j] - col), mates[j], 5 + j).start()
+
+    def pass_far():
+        send_in(0, 0, me + COLS, 4).wait_recv()
+        for j in range(3):
+            @pl.when(cols[j] < col)
+            def _():
+                send_in(0, col - cols[j], mates[j], 1 + j).start()
+
+    def send_out(back, target):
+        near = jnp.where((back > col) & (back <= col + COLS), 0, 1)
+        at = back % COLS - 1
+        return pltpu.make_async_remote_copy(
+            src_ref=part.at[REACH - back], dst_ref=from_mates.at[near, at],
+            send_sem=out_send.at[back], recv_sem=out_recv.at[near, at],
+            device_id=place(target), device_id_type=MESH,
+        )
+
+    def mate_arrival(kind, j):
+        return pltpu.make_async_remote_copy(
+            src_ref=part.at[0], dst_ref=from_mates.at[kind, j],
+            send_sem=out_send.at[1], recv_sem=out_recv.at[kind, j],
+            device_id=place(mates[j]), device_id_type=MESH,
+        )
+
+    def send_sum(source, dest, target, index):
+        return pltpu.make_async_remote_copy(
+            src_ref=source, dst_ref=dest, send_sem=out_send.at[index], recv_sem=out_recv.at[index // 4 - 1, 3],
+            device_id=place(target), device_id_type=MESH,
+        )
+
+    near_send = send_sum(sum_near, from_near, me - COLS, 4)
+    far_send = send_sum(sum_far, from_far, me - REACH, 8)
+
+    def flush(step):
+        back = back_of(step, col)
+        slot = REACH - back
+
+        @pl.when(step <= REACH)
+        def _():
+            part[slot, 0] = (acc[slot, 0] * SCALE).astype(BF16)
+            part[slot, 1] = acc[slot, 1].astype(BF16)
+
+        @pl.when((back != 0) & (back != 4) & (back != 8))
+        def _():
+            send_out(back, me - col + (col - back + 2 * COLS) % COLS).start()
+
+    def exchange(phase, source, dest, along_lo):
+        def copy(i, arriving):
+            base = lo if along_lo else hi
+            index = (base + i) % LO
+            target = (hi, index) if along_lo else (index, lo)
+            mine = index if arriving else base
+            return pltpu.make_async_remote_copy(
+                src_ref=source(index), dst_ref=dest(mine),
+                send_sem=s_send.at[phase, i], recv_sem=s_recv.at[phase, mine],
+                device_id=target, device_id_type=MESH,
+            )
+
+        def start():
+            def body(i, carry):
+                copy(i, False).start()
+                return carry
+            lax.fori_loop(1, LO, body, 0)
+
+        def finish():
+            def body(i, carry):
+                copy(i, True).wait_recv()
+                copy(i, False).wait_send()
+                return carry
+            lax.fori_loop(1, LO, body, 0)
+
+        return start, finish
+
+    start1, finish1 = exchange(0, lambda i: sink_parts.at[i], lambda i: sink_in.at[i], True)
+    start2, finish2 = exchange(1, lambda i: sink_sum, lambda i: sink_mid.at[i], False)
+    start3, finish3 = exchange(2, lambda i: sink_buf, lambda i: sink_all.at[i], True)
+
+    def sum_of(ref):
+        def body(i, total):
+            return total + ref[i]
+        return lax.fori_loop(1, LO, body, ref[0])
+
+    def sink_begin():
+        half = LO // 2
+        sink_parts[:half] = (acc[SINK_SLOT, 0, :, :DH] * SCALE).reshape(half, piece, DH)
+        sink_parts[half:] = acc[SINK_SLOT, 1, :, :DH].reshape(half, piece, DH)
+        start1()
+
+    def sink_second():
+        finish1()
+        sink_in[lo] = sink_parts[lo]
+        sink_sum[...] = sum_of(sink_in)
+        start2()
+
+    def sink_third():
+        finish2()
+        sink_mid[hi] = sink_sum[...]
+        sink_buf[...] = sum_of(sink_mid)
+        start3()
+
+    lax.fori_loop(EARLY, HEADS, prepare, 0)
 
     def slot_of(step):
         return jnp.where(step == 0, SINK_SLOT, REACH - back_of(step, col))
@@ -310,11 +312,11 @@
             def _():
                 sink_begin()
 
-            @pl.when(step == 3)
+            @pl.when(step == 4)
             def _():
                 sink_second()
 
-            @pl.when(step == 5)
+            @pl.when(step == 7)
             def _():
                 sink_third()
 

time: 67.1 us -> 66.5 us (level)
  Pallas kernels: 66.3 us -> 65.2 us
    pallas_call x1, Pallas kernels: 64.8 us -> 63.8 us  [fused(): pl.pallas_call(fused_kernel, out_shape=(jax.ShapeDtypeStruct((TOK, HEADS...]
where the time goes in v6:
time: 66.5 us; the launch traced here: 65.9 us
  Pallas kernels  65.2 us (98%)
    pallas_call x1, Pallas kernels, fused(): pl.pallas_call(fused_kernel, out_shape=(jax.ShapeDtypeStruct((TOK, HEADS...  63.8 us
    pallas_call x1, Pallas kernels, finish(): pl.pallas_call(finish_kernel, out_shape=[jax.ShapeDtypeStruct(x.shape, F3...  1.47 us

profile of v6, /device:TPU:32, one launch (start us, length us, event | category | flops | bytes accessed | tf_op | source)
XLA Modules:
  0.0 65.9 jit_solution(729668162569041839)
XLA Ops:
  0.6 63.8 %window_backward.1 = (f32[256,2048]{1,0:T(8,128)S(1)}, f32[256,128]{1,0:T(8,128)S(1)}, f32[256,128]{1,0:T(8,128)S(1)}, f32[128,128]{1,0:T(8,128)S(1)}, f32[128,128]{1,0:T(8,128)S(1)}) custom-call(s32[16]{0:T(128)} %window.1, s32[16]{0:T(128)} %live.1, bf16[256,2048]{1,0:T(8,128)(2,1)} %q_hbm.1, bf16[256,2048]{1,0:T(8,128)(2,1)} %o_hbm.1, ...), custom_call_target="tpu_custom_call" | custom-call | tf_op jit(solution)/shard_map/window_backward/pallas_call | solution.py:413
  64.4 1.5 %finish.1 = (f32[256,2048]{1,0:T(8,128)}, f32[256,128]{1,0:T(8,128)}, f32[256,128]{1,0:T(8,128)}, f32[128,128]{1,0:T(8,128)}, f32[128,128]{1,0:T(8,128)}) custom-call(f32[256,2048]{1,0:T(8,128)S(1)} %get-tuple-element.10.refs_0_, f32[256,128]{1,0:T(8,128)S(1)} %get-tuple-element.11.refs_1_, f32[256,128]{1,0:T(8,128)S(1)} %get-tuple-element.12.refs_2_, ...), custom_call_target="tpu_custom_call" | custom-call | tf_op jit(solution)/shard_map/finish/pallas_call | solution.py:482
